TPU v7x, 32 devices: a whole 2x2x4 slice. The times are simulated.
32 devices in a mesh: ctx: 8 (over z, x), tp: 4 (over y, core).
Axes of the slice: x: 2, y: 2, z: 4, core: 2. Of those that a mesh axis runs over, the one named last changes fastest.
Arguments:
- resid: bfloat16 [1024, 8192], P('ctx', 'tp'), may hold values from -64 to 64
- q_mr: bfloat16 [1024, 8192], P('ctx', 'tp'), may hold values from -4 to 4
- k_mr: bfloat16 [1024, 8192], P('ctx', 'tp'), may hold values from -4 to 4
- v_mr: bfloat16 [1024, 8192], P('ctx', 'tp'), may hold values from -4 to 4
- mr_taps: bfloat16 [512, 128], P('tp'), may hold values from -0.5 to 0.5
- norm_gain: bfloat16 [8192], P('tp'), may hold values from 0.099609375 to 1.8984375
- q_lr: bfloat16 [1024, 8192], P('ctx', 'tp'), may hold values from -4 to 4
- k_lr: bfloat16 [1024, 8192], P('ctx', 'tp'), may hold values from -4 to 4
- pole_rate: float32 [16, 512], P(None, 'tp'), may hold values from 0 to 1, as said below
- residue: float32 [16, 512], P(None, 'tp'), may hold values from -3 to 3
Outputs:
- mixed: bfloat16 [1024, 8192], P('ctx', 'tp')
- lr_out: bfloat16 [1024, 8192], P('ctx', 'tp')
Inputs may be any that keep to these rules, and one draw needn't show every extreme that they name: `pole_rate`: every rate is positive.
All inputs are finite; a program needn't handle non-finite values.
Results may differ from a plain program's by a relative error of at most 0.0052.
Values may be sent and summed in bfloat16 or wider, within the bound.
No kernel may reach another device: no remote copies, remote signals or barrier semaphores. Data moves between devices by JAX's collectives and lax.ppermute only.
A program may use at most 128 MiB of HBM per device.

v0:
```python
import jax
import jax.numpy as jnp
from jax import lax
from jax.sharding import PartitionSpec as P

D = 8192


HIGHEST_MODE = lax.Precision.HIGHEST


def passed_along(x, axis, by):
    peers = lax.axis_size(axis)
    pairs = [(i, i + by) for i in range(peers) if 0 <= i + by < peers]
    return lax.ppermute(x, axis, pairs)


def carried_in(part, axis, combine, identity):
    place = lax.axis_index(axis)
    gathered = jax.tree.map(lambda a: lax.all_gather(a, axis), part)
    state = jax.tree.map(lambda a, e: jnp.zeros_like(a) + jnp.asarray(e, a.dtype), part, identity)

    def one(step, state):
        return combine(
            state, jax.tree.map(lambda a: lax.dynamic_index_in_dim(a, step, 0, False), gathered)
        )

    return lax.fori_loop(0, place, one, state)


def banded(vector, out_rows):
    length = vector.shape[-1]
    span_cols = out_rows + length - 1
    padding = jnp.zeros(vector.shape[:-1] + (span_cols + 1 - length,), vector.dtype)
    line = jnp.concatenate([vector, padding], axis=-1)
    tiled = jnp.tile(line, (1,) * (vector.ndim - 1) + (out_rows,))
    return tiled[..., : out_rows * span_cols].reshape(vector.shape[:-1] + (out_rows, span_cols))


def modal_tables(pole_rate, residue, tok_rows):
    weights_eff = residue * jnp.sqrt(-jnp.expm1(-2.0 * pole_rate))
    positions = jnp.arange(tok_rows, dtype=jnp.float32)
    powers = jnp.exp(-pole_rate[:, :, None] * positions)
    impulse = jnp.sum(weights_eff[:, :, None] * powers, axis=0)
    square = banded(impulse[:, ::-1], tok_rows)[:, :, tok_rows - 1 :]
    entry = weights_eff[:, :, None] * powers * jnp.exp(-pole_rate)[:, :, None]
    leaving = powers[:, :, ::-1]
    through = jnp.exp(-pole_rate * tok_rows)
    return (square, entry, leaving, through)


def tokens_last(rows, local_groups, group_size):
    row_count = rows.shape[0]
    return jnp.transpose(rows.reshape(row_count, local_groups, group_size), (1, 2, 0))


def tokens_first(grouped, channels):
    return jnp.transpose(grouped, (2, 0, 1)).reshape(grouped.shape[2], channels)


def per_device(resid, q_mr, k_mr, v_mr, mr_taps, norm_gain, q_lr, k_lr, pole_rate, residue):
    tok_rows, channels = resid.shape
    local_groups, tap_count = mr_taps.shape
    group_size = channels // local_groups
    mr_in = (k_mr.astype(jnp.float32) * v_mr.astype(jnp.float32)).astype(jnp.bfloat16)
    rim_rows = passed_along(mr_in[tok_rows - tap_count + 1 :], "ctx", 1)
    window = jnp.concatenate([rim_rows, mr_in], axis=0)
    window = tokens_last(window, local_groups, group_size)
    kernel = banded(mr_taps[:, ::-1], tok_rows)
    mr_conv = jnp.einsum("gtr,gcr->gct", kernel, window, preferred_element_type=jnp.float32)
    mr_conv = tokens_first(mr_conv, channels)
    mixed = (resid.astype(jnp.float32) + q_mr.astype(jnp.float32) * mr_conv).astype(jnp.bfloat16)
    mixed_f = mixed.astype(jnp.float32)
    square_sum = lax.psum(jnp.sum(mixed_f * mixed_f, axis=1), "tp")
    normed = mixed_f * lax.rsqrt(square_sum[:, None] / D + 1e-06) * norm_gain.astype(jnp.float32)
    lr_in = tokens_last(k_lr.astype(jnp.float32) * normed, local_groups, group_size)
    square, entry, leaving, through = modal_tables(pole_rate, residue, tok_rows)
    local = jnp.einsum("gts,gcs->gct", square, lr_in, precision=HIGHEST_MODE)
    state_end = jnp.einsum("pgs,gcs->pgc", leaving, lr_in, precision=HIGHEST_MODE)
    state_end = state_end.reshape(state_end.shape[0], channels)

    def combine(former, latter):
        factor = jnp.repeat(latter[0], group_size, axis=1)
        return (former[0] * latter[0], factor * former[1] + latter[1])

    identity = (jnp.ones_like(through), jnp.zeros_like(state_end))
    scanned = carried_in((through, state_end), "ctx", combine, identity)
    carried = scanned[1]
    carried = carried.reshape(carried.shape[0], local_groups, group_size)
    incoming = jnp.einsum("pgt,pgc->gct", entry, carried, precision=HIGHEST_MODE)
    lr_conv = tokens_first(local + incoming, channels)
    lr_out = (q_lr.astype(jnp.float32) * lr_conv).astype(jnp.bfloat16)
    return (mixed, lr_out)


def solution(mesh):
    placed = (
        P("ctx", "tp"),
        P("ctx", "tp"),
        P("ctx", "tp"),
        P("ctx", "tp"),
        P("tp", None),
        P("tp"),
        P("ctx", "tp"),
        P("ctx", "tp"),
        P(None, "tp"),
        P(None, "tp"),
    )
    return jax.shard_map(
        per_device,
        mesh=mesh,
        in_specs=placed,
        out_specs=(P("ctx", "tp"), P("ctx", "tp")),
        check_vma=False,
    )
```

profile of v0, /device:TPU:26, one launch (start us, length us, event | category | flops | bytes accessed | tf_op | source)
XLA Modules:
  0.0 223.1 jit_solution(2459947831379323404)
XLA Ops:
  7.2 1.3 multiply_convert_fusion.1
  8.5 0.9 slice.16
  9.5 1.3 collective-permute-start
  13.7 3.8 %tile.8 = bf16[128,128,256]{2,1,0:T(8,128)(2,1)} broadcast(bf16[128,256]{1,0:T(8,128)(2,1)S(1)} %concatenate.10), dimensions={0,2} | broadcast | bytes 8454144 | tf_op jit(solution)/shard_map/tile | solution.py:36
  17.5 12.3 %copy.44 = bf16[16,8,128,256]{3,1,2,0:T(8,128)(2,1)} copy(bf16[16,8,128,256]{3,2,1,0:T(8,128)(2,1)} %bitcast.43) | data formatting | bytes 16777216
  29.8 7.1 %slice.17 = bf16[128,32640]{1,0:T(8,128)(2,1)} slice(bf16[128,32768]{1,0:T(8,128)(2,1)} %bitcast.44), slice={[0:128], [0:32640]} | slice | bytes 16711680 | tf_op jit(solution)/shard_map/slice | solution.py:37
  37.0 29.6 %reshape.47 = bf16[128,128,255]{2,1,0:T(8,128)(2,1)} reshape(bf16[128,32640]{1,0:T(8,128)(2,1)} %slice.17) | data formatting | bytes 16711680 | tf_op jit(solution)/shard_map/reshape | solution.py:37
  66.6 1.0 copy.32
  67.6 1.0 copy.33
  68.9 2.2 %pad_maximum_fusion = bf16[255,2048]{1,0:T(8,128)(2,1)} fusion(bf16[128,2048]{1,0:T(8,128)(2,1)S(1)} %multiply_convert_fusion.1, bf16[127,2048]{1,0:T(8,128)(2,1)} %collective-permute-done), kind=kLoop, calls=%fused_computation.10 | loop fusion | flops 2088960 | bytes 2088960 | tf_op jit(solution)/shard_map/concatenate | solution.py:67
  71.1 1.5 copy.34
  72.6 5.7 %fusion.13 = f32[128,16,128]{2,1,0:T(8,128)S(1)} fusion(bf16[128,16,255]{2,1,0:T(8,128)(2,1)S(1)} %bitcast.49, bf16[128,128,255]{2,1,0:T(8,128)(2,1)} %reshape.47), kind=kOutput, calls=%fused_computation.27 | convolution fusion | flops 133693440 | bytes 10448896 | tf_op jit(solution)/shard_map/gtr,gcr->gct/dot_general | solution.py:70
  78.7 7.1 %psum.7 = f32[128]{0:T(128)S(1)} all-reduce(f32[128]{0:T(128)S(1)} %get-tuple-element.61), channel_id=1, replica_groups=mesh['ctx'=8,'tp'=4] {'tp'}, use_global_device_ids=true, to_apply=%region_1.0 | all-reduce | flops 128 | bytes 1024 | tf_op jit(solution)/shard_map/psum | solution.py:74
  86.1 2.7 %fusion.14 = f32[128,16,16]{2,1,0:T(8,128)} fusion(f32[128,16,128]{2,1,0:T(8,128)S(1)} %bitcast.45, f32[16,128,128]{2,0,1:T(8,128)S(1)} %rev.11), kind=kOutput, calls=%fused_computation.28 | convolution fusion | flops 50331648 | bytes 2228224 | tf_op jit(solution)/shard_map/pgs,gcs->pgc/dot_general | solution.py:79
  88.8 2.2 copy.38
  91.2 1.3 tile.20
  92.5 20.7 %copy.45 = f32[16,8,128,256]{3,1,2,0:T(8,128)S(1)} copy(f32[16,8,128,256]{3,2,1,0:T(8,128)S(1)} %bitcast.41) | data formatting | bytes 33554432
  113.2 6.0 %slice.18 = f32[128,32640]{1,0:T(8,128)} slice(f32[128,32768]{1,0:T(8,128)S(1)} %bitcast.42), slice={[0:128], [0:32640]} | slice | bytes 33423360 | tf_op jit(solution)/shard_map/slice | solution.py:37
  119.2 28.9 %reshape.50 = f32[128,128,255]{2,1,0:T(8,128)} reshape(f32[128,32640]{1,0:T(8,128)} %slice.18) | data formatting | bytes 33423360 | tf_op jit(solution)/shard_map/reshape | solution.py:37
  148.8 30.5 %all-gather = f32[128,128]{1,0:T(8,128)S(1)} all-gather(f32[16,128]{1,0:T(8,128)S(1)} %get-tuple-element.66), channel_id=2, replica_groups=mesh['ctx'=8,'tp'=4] {'ctx'}, dimensions={0}, use_global_device_ids=true | all-gather | bytes 73728 | tf_op jit(solution)/shard_map/all_gather | solution.py:20
  179.4 1.0 copy.42
  180.4 16.2 %fusion = f32[128,16,128]{2,1,0:T(8,128)S(1)} fusion(f32[128,16,128]{2,1,0:T(8,128)S(1)} %bitcast.46, f32[128,128,255]{2,1,0:T(8,128)} %reshape.50), kind=kOutput, calls=%fused_computation.2 | convolution fusion | flops 402653184 | bytes 10485760 | tf_op jit(solution)/shard_map/gts,gcs->gct/dot_general | solution.py:78
  196.6 13.8 %while.12 = (s32[]{:T(128)}, f32[16,2048]{1,0:T(8,128)S(1)}, s32[]{:T(128)}, f32[8,16,128]{2,1,0:T(8,128)S(1)}, f32[8,16,2048]{2,1,0:T(8,128)}, /*index=5*/s32[]{:T(128)}, s32[]{:T(128)}, s32[]{:T(128)}) while((s32[]{:T(128)}, f32[16,2048]{1,0:T(8,128)S(1)}, s32[]{:T(128)}, f32[8,16,128]{2,1,0:T(8,128)S(1)}, f32[8,16,2048]{2,1,0:T(8,128)}, ...), condition=%wide.region_4.5_spmd, body=%wide.region_3.4_spmd.sunk | while | flops 65541 | bytes 942207 | solution.py:28
  197.6 1.0 bitcast_add_fusion.2
  199.6 1.0 bitcast_add_fusion.2
  201.6 1.0 bitcast_add_fusion.2
  203.5 1.0 bitcast_add_fusion.2
  205.5 1.0 bitcast_add_fusion.2
  207.5 1.0 bitcast_add_fusion.2
  209.5 1.0 bitcast_add_fusion.2
  210.8 3.2 %convolution_add_fusion = f32[128,16,128]{2,1,0:T(8,128)S(1)} fusion(f32[128,16,128]{2,1,0:T(8,128)S(1)} %fusion, f32[16,128,16]{0,2,1:T(8,128)S(1)} %bitcast.47, f32[16,128]{0,1:T(8,128)} %copy.39, f32[16,128]{0,1:T(8,128)S(1)} %copy.37, f32[16,128]{0,1:T(8,128)S(1)} %copy.36), kind=kOutput, calls=%fused_computation.4 | convolution fusion | flops 51380224 | bytes 2252800 | tf_op jit(solution)/shard_map/pgt,pgc->gct/dot_general | solution.py:90
  214.3 1.9 multiply_convert_fusion
  (55 shorter events, 12.2 us)
Async XLA Ops:
  7.2 189.4 %all-gather.3.cloned.1.call-start = ((), (), s32[]{:S(2)}) async-start(), calls=%async_computation | async-start | bytes 1179648 | tf_op jit(solution)/shard_map/all_gather | solution.py:20
  9.5 59.4 %collective-permute-start = (bf16[127,2048]{1,0:T(8,128)(2,1)}, bf16[127,2048]{1,0:T(8,128)(2,1)}, u32[]{:S(2)}, u32[]{:S(2)}) collective-permute-start(bf16[127,2048]{1,0:T(8,128)(2,1)} %slice.16), channel_id=1, source_target_pairs={{0,4},{4,8},{8,12},{12,16},{16,20},{20,24},{24,28},{1,5},{5,9},{9,... | collective-permute-start | bytes 1560584 | tf_op jit(solution)/shard_map/ppermute | solution.py:15
  37.0 29.6 %copy-start.2 = (bf16[128,2048]{1,0:T(8,128)(2,1)S(1)}, bf16[128,2048]{1,0:T(8,128)(2,1)}, u32[]{:S(2)}) copy-start(bf16[128,2048]{1,0:T(8,128)(2,1)} %param.12) | copy-start | bytes 1572868
  37.0 30.6 %copy-start.3 = (bf16[128,2048]{1,0:T(8,128)(2,1)S(1)}, bf16[128,2048]{1,0:T(8,128)(2,1)}, u32[]{:S(2)}) copy-start(bf16[128,2048]{1,0:T(8,128)(2,1)} %param.13) | copy-start | bytes 1572868
  37.0 31.6 %copy-start.4 = (bf16[128,2048]{1,0:T(8,128)(2,1)S(1)}, bf16[128,2048]{1,0:T(8,128)(2,1)}, u32[]{:S(2)}) copy-start(bf16[128,2048]{1,0:T(8,128)(2,1)} %param.19) | copy-start | bytes 1572868
  37.0 31.9 %copy-start.5 = (bf16[2048]{0:T(1024)(128)(2,1)S(1)}, bf16[2048]{0:T(1024)(128)(2,1)}, u32[]{:S(2)}) copy-start(bf16[2048]{0:T(1024)(128)(2,1)} %param.17) | copy-start | bytes 12292
  72.6 5.7 %copy-start = (bf16[128,2048]{0,1:T(8,128)(2,1)S(1)}, bf16[128,2048]{0,1:T(8,128)(2,1)}, u32[]{:S(2)}) copy-start(bf16[128,2048]{0,1:T(8,128)(2,1)} %copy.32) | copy-start | bytes 1572868
  72.6 5.7 %copy-start.1 = (bf16[128,2048]{0,1:T(8,128)(2,1)S(1)}, bf16[128,2048]{0,1:T(8,128)(2,1)}, u32[]{:S(2)}) copy-start(bf16[128,2048]{0,1:T(8,128)(2,1)} %copy.33) | copy-start | bytes 1572868
Sparse Core Ops, SparseCore 0:
  91.2 39.1 all-gather.2
where the time goes:
time: 224 us; the launch traced here: 223 us
  local copies, waits for them, and re-layouts  127 us (57%)
  blocking collectives  37.6 us (17%)
  matrix products  27.9 us (12%)
  other arithmetic  14.4 us (6%)
  between operations  14.2 us (6%)
    reshape x2, local copies, waits for them, and re-layouts, banded(): tiled[..., :out_rows * span_cols]  58.5 us
    unnamed x18, local copies, waits for them, and re-layouts  36.3 us
    all_gather x1, blocking collectives, carried_in(): gathered = jax.tree.map(lambda a: lax.all_gather(a, axis), part)  30.5 us
    dot_general x1, matrix products, per_device(): local = jnp.einsum('gts,gcs->gct', square, lr_in, precision=HIGHEST_MODE)  16.2 us
    slice x2, local copies, waits for them, and re-layouts, banded(): tiled[..., :out_rows * span_cols]  13.1 us
    psum x1, blocking collectives, per_device(): square_sum = lax.psum(jnp.sum(mixed_f * mixed_f, axis=1), 'tp')  7.1 us
    add x7, other arithmetic, combine(): return (former[0] * latter[0], factor * former[1] + latter[1])  6.8 us
    dot_general x1, matrix products, per_device(): jnp.einsum('gtr,gcr->gct', kernel, window, preferred_element_type=jnp.flo...  5.72 us
  transfers between devices with their start and end apart: 2, of which 0 were waited for; matrix products, arithmetic and copies ran while one was open for 60% of the time, Pallas kernels for 0%

commit v1 on v0

v1 whole, which is shorter than its diff:
```python
import functools

import jax
import jax.numpy as jnp
from jax import lax
from jax.experimental import pallas as pl
from jax.experimental.pallas import tpu as pltpu
from jax.sharding import PartitionSpec as P

LANES = 128
F32, BF16 = jnp.float32, jnp.bfloat16
VMEM = pl.BlockSpec(memory_space=pltpu.VMEM)


def shifted(x, axis, by):
    peers = lax.axis_size(axis)
    return lax.ppermute(x, axis, [(i, i + by) for i in range(peers) if i + by < peers])


def swapped(x, axis, bit):
    peers = lax.axis_size(axis)
    return lax.ppermute(x, axis, [(i, i ^ bit) for i in range(peers) if i ^ bit < peers])


def everyone(x, axis):
    peers = lax.axis_size(axis)
    if peers & (peers - 1) == 0:
        return [x] + [swapped(x, axis, bit) for bit in range(1, peers)]
    turns = [[(i, (i + by) % peers) for i in range(peers)] for by in range(1, peers)]
    return [x] + [lax.ppermute(x, axis, turn) for turn in turns]


def lane_group(shape, width):
    return lax.broadcasted_iota(jnp.int32, shape, 1) // width


def by_parity(x, group_size):
    odd = jnp.where(lane_group((1, LANES), group_size) % 2 == 1, 1.0, 0.0)
    return jnp.concatenate([x * (1.0 - odd).astype(x.dtype), x * odd.astype(x.dtype)], axis=0)


def own_lanes(stacked, group_size):
    pairs = LANES // (2 * group_size)
    rows = stacked.shape[0] // pairs
    pair_of = lane_group((rows, LANES), 2 * group_size)
    out = stacked[:rows]
    for pair in range(1, pairs):
        out = jnp.where(pair_of == pair, stacked[pair * rows : (pair + 1) * rows], out)
    return out


def matmul(a, b):
    return jnp.dot(a, b, preferred_element_type=F32)


def turned(row, size):
    return pltpu.roll(jnp.broadcast_to(row, (size, size)), 0, 1, stride=1, stride_axis=0)


def over_tiles(channels, body, init=0):
    return lax.fori_loop(0, channels // LANES, body, init)


def tile_of(i):
    return pl.ds(pl.multiple_of(i * LANES, LANES), LANES)


def prep_kernel(
    group_size, u_ref, taps_ref, rate_ref, weight_ref,
    acc_ref, upper_ref, square_ref, leave_ref, entry_ref, rev, lhs, enter,
):
    tok, channels = u_ref.shape
    poles, groups = rate_ref.shape
    per = LANES // group_size
    row = lax.broadcasted_iota(jnp.int32, (tok, tok), 0)
    col = lax.broadcasted_iota(jnp.int32, (tok, tok), 1)
    total = row + col
    flip = jnp.where((total == 0) | (total == tok), 1.0, 0.0).astype(BF16)
    rev[...] = matmul(taps_ref[...], flip)
    position = lax.broadcasted_iota(jnp.int32, (poles, tok), 1)
    back = jnp.where(position == 0, 0, tok - position).astype(F32)
    ahead = (position + 1).astype(F32)
    remain = (tok - 1 - position).astype(F32)

    def body(i, _):
        causal = row >= col
        turn = lax.rem(groups - i * per, groups)
        rate = pltpu.roll(rate_ref[...], turn, 1)
        weight = pltpu.roll(weight_ref[...], turn, 1)
        for k in range(per):
            pair, half = k // 2, k % 2
            rows, cols = pl.ds(pair * tok, tok), pl.ds(half * tok, tok)
            ring = turned(rev[pl.ds(i * per + k, 1), :], tok)
            lhs[rows, cols] = jnp.where(causal, ring, 0.0).astype(BF16)
            upper_ref[i, rows, cols] = jnp.where(causal, 0.0, ring).astype(BF16)
            rate_k = jnp.broadcast_to(rate[:, k : k + 1], (poles, tok))
            weight_k = jnp.broadcast_to(weight[:, k : k + 1], (poles, tok))
            impulse = jnp.sum(weight_k * jnp.exp(-rate_k * back), axis=0, keepdims=True)
            ring = turned(impulse, tok)
            square_ref[i, rows, cols] = jnp.where(causal, ring, 0.0).astype(BF16)
            leave_ref[i, pl.ds(pair * poles, poles), cols] = jnp.exp(-rate_k * remain)
            enter[pl.ds(k * poles, poles), :] = weight_k * jnp.exp(-rate_k * ahead)
        entry_ref[i] = enter[...].T.astype(BF16)
        x = by_parity(u_ref[:, tile_of(i)], group_size)
        acc_ref[:, tile_of(i)] = own_lanes(matmul(lhs[...], x), group_size)
        return 0

    over_tiles(channels, body)


def mix_kernel(
    group_size, halo_ref, acc_ref, upper_ref, resid_ref, q_ref, k_ref, gain_ref,
    mixed_ref, z_ref, zb_ref, sum_ref,
):
    tok, channels = halo_ref.shape

    def body(i, total):
        at = tile_of(i)
        past = own_lanes(matmul(upper_ref[i], by_parity(halo_ref[:, at], group_size)), group_size)
        conv = acc_ref[:, at] + past
        mixed = (resid_ref[:, at].astype(F32) + q_ref[:, at].astype(F32) * conv).astype(BF16)
        mixed_ref[:, at] = mixed
        mixed = mixed.astype(F32)
        z = k_ref[:, at].astype(F32) * mixed * gain_ref[:, at].astype(F32)
        z_ref[:, at] = z
        zb_ref[i] = by_parity(z.astype(BF16), group_size)
        return total + mixed * mixed

    total = over_tiles(channels, body, jnp.zeros((tok, LANES), F32))
    sum_ref[...] = jnp.sum(total.T, axis=0, keepdims=True)


def state_kernel(group_size, width, parts, *refs):
    sums, (leave_ref, zb_ref, state_ref, scale_ref) = refs[:parts], refs[parts:]
    square_sum = sums[0][...]
    for other in sums[1:]:
        square_sum = square_sum + other[...]
    scale = lax.rsqrt(square_sum / width + 1e-06)
    scale_ref[...] = scale
    twice = jnp.concatenate([scale, scale], axis=1)
    channels = state_ref.shape[1]

    def body(i, _):
        leaving = (leave_ref[i] * twice).astype(BF16)
        state_ref[:, tile_of(i)] = own_lanes(matmul(leaving, zb_ref[i]), group_size)
        return 0

    over_tiles(channels, body)


def local_kernel(group_size, scale_ref, z_ref, square_ref, local_ref):
    tok, channels = z_ref.shape
    scale = jnp.broadcast_to(scale_ref[...], (LANES, tok)).T

    def body(i, _):
        y = by_parity((z_ref[:, tile_of(i)] * scale).astype(BF16), group_size)
        local_ref[:, tile_of(i)] = own_lanes(matmul(square_ref[i], y), group_size)
        return 0

    over_tiles(channels, body)


def final_kernel(group_size, rounds, *refs):
    got, factors = refs[:rounds], refs[rounds : 2 * rounds]
    entry_ref, local_ref, q_ref, out_ref = refs[2 * rounds :]
    poles, channels = got[0].shape
    per = LANES // group_size
    group_of = lane_group((poles, LANES), group_size)

    def body(i, _):
        at = tile_of(i)
        carried = jnp.zeros((poles, LANES), F32)
        for state, factor in zip(got, factors):
            carried = carried + factor[:, at] * state[:, at].astype(F32)
        spread = jnp.concatenate([jnp.where(group_of == g, carried, 0.0) for g in range(per)], axis=0)
        conv = local_ref[:, at] + matmul(entry_ref[i], spread.astype(BF16))
        out_ref[:, at] = (q_ref[:, at].astype(F32) * conv).astype(BF16)
        return 0

    over_tiles(channels, body)


def held(shape, dtype):
    return jax.ShapeDtypeStruct(shape, dtype)


def call(kernel, outs, scratch, flops, *args):
    size = sum(a.size * a.dtype.itemsize for a in args)
    return pl.pallas_call(
        kernel,
        out_shape=outs,
        in_specs=[VMEM] * len(args),
        out_specs=jax.tree.map(lambda _: VMEM, outs),
        scratch_shapes=scratch,
        cost_estimate=pl.CostEstimate(flops=flops, bytes_accessed=size, transcendentals=0),
    )(*args)


def per_device(resid, q_mr, k_mr, v_mr, mr_taps, norm_gain, q_lr, k_lr, pole_rate, residue):
    tok, channels = resid.shape
    groups, tap_count = mr_taps.shape
    poles = pole_rate.shape[0]
    group_size = channels // groups
    assert tap_count == tok and channels % LANES == 0 and LANES % (2 * group_size) == 0
    tiles, pairs = channels // LANES, LANES // (2 * group_size)
    width = channels * lax.axis_size("tp")
    shards = lax.axis_size("ctx")
    place = lax.axis_index("ctx")
    bits = [1 << b for b in range((shards - 1).bit_length())]
    stacked = (tiles, pairs * tok, 2 * tok)
    work = 2 * tok * tok * channels * pairs * 2

    u = (k_mr.astype(F32) * v_mr.astype(F32)).astype(BF16)
    halo = shifted(u, "ctx", 1)

    weights = residue * jnp.sqrt(-jnp.expm1(-2.0 * pole_rate))
    acc, upper, square, leave, entry = call(
        functools.partial(prep_kernel, group_size),
        (
            held((tok, channels), F32),
            held(stacked, BF16),
            held(stacked, BF16),
            held((tiles, pairs * poles, 2 * tok), F32),
            held((tiles, tok, LANES // group_size * poles), BF16),
        ),
        [
            pltpu.VMEM((groups, tok), F32),
            pltpu.VMEM(stacked[1:], BF16),
            pltpu.VMEM((LANES // group_size * poles, tok), F32),
        ],
        4 * work,
        u, mr_taps, pole_rate, weights,
    )
    rate = jnp.repeat(pole_rate, group_size, axis=1) * tok
    factors, keeps, takes = [], [], []
    for bit in bits:
        late = (place & bit) != 0
        behind = (place & (bit - 1)).astype(F32)
        factors.append(jnp.where(late, jnp.exp(-rate * behind), 0.0))
        whole = jnp.exp(-rate * bit)
        keeps.append(jnp.where(late, 1.0, whole))
        takes.append(jnp.where(late, whole, 1.0))

    mixed, z, zb, square_sum = call(
        functools.partial(mix_kernel, group_size),
        (
            held((tok, channels), BF16),
            held((tok, channels), F32),
            held((tiles, 2 * tok, LANES), BF16),
            held((1, tok), F32),
        ),
        [],
        work,
        halo, acc, upper, resid, q_mr, k_lr, norm_gain.reshape(1, channels),
    )
    sums = everyone(square_sum, "tp")
    state, scale = call(
        functools.partial(state_kernel, group_size, width, len(sums)),
        (held((poles, channels), F32), held((1, tok), F32)),
        [],
        work // 8,
        *sums, leave, zb,
    )
    local = call(
        functools.partial(local_kernel, group_size),
        held((tok, channels), F32),
        [],
        work,
        scale, z, square,
    )
    got = []
    for step, bit in enumerate(bits):
        got.append(swapped(state.astype(BF16), "ctx", bit))
        state = keeps[step] * state + takes[step] * got[step].astype(F32)
    lr_out = call(
        functools.partial(final_kernel, group_size, len(bits)),
        held((tok, channels), BF16),
        [],
        work // 8,
        *got, *factors, entry, local, q_lr,
    )
    return (mixed, lr_out)


def solution(mesh):
    whole, tables = P("ctx", "tp"), P(None, "tp")
    placed = (whole,) * 4 + (P("tp", None), P("tp")) + (whole,) * 2 + (tables,) * 2
    return jax.shard_map(
        per_device, mesh=mesh, in_specs=placed, out_specs=(whole, whole), check_vma=False
    )
```

time: 224 us -> 73.8 us (0.33)
  the two profiles are of different devices: /device:TPU:26 before, /device:TPU:0 now
where the time goes in v1:
time: 73.8 us; the launch traced here: 73.5 us
  Pallas kernels  40.2 us (54%)
  starting transfers between devices  12.5 us (17%)
  local copies, waits for them, and re-layouts  11.9 us (16%)
  waiting for transfers between devices  4.45 us (6%)
  other arithmetic  3.7 us (5%)
  between operations  0.76 us (1%)
    pallas_call x5, Pallas kernels, call(): pl.pallas_call(kernel, out_shape=outs, in_specs=[VMEM] * len(args), out_s...  40.2 us
    ppermute x6, starting transfers between devices, swapped(): lax.ppermute(x, axis, [(i, i ^ bit) for i in range(peers) if i ^ bit < pe...  7.61 us
    ppermute x1, starting transfers between devices, shifted(): lax.ppermute(x, axis, [(i, i + by) for i in range(peers) if i + by < peers])  4.9 us
    ppermute x6, waiting for transfers between devices, swapped(): lax.ppermute(x, axis, [(i, i ^ bit) for i in range(peers) if i ^ bit < pe...  4.45 us
    select_n x3, local copies, waits for them, and re-layouts, per_device(): factors.append(jnp.where(late, jnp.exp(-rate * behind), 0.0))  3.87 us
    broadcast_in_dim x7, local copies, waits for them, and re-layouts, per_device(): rate = jnp.repeat(pole_rate, group_size, axis=1) * tok  2.26 us
    unnamed x18, local copies, waits for them, and re-layouts  1.92 us
  transfers between devices with their start and end apart: 7, of which 4 were waited for; matrix products, arithmetic and copies ran while one was open for 15% of the time, Pallas kernels for 30%

profile of v1, /device:TPU:0, one launch (start us, length us, event | category | flops | bytes accessed | tf_op | source)
XLA Modules:
  0.0 73.5 jit_solution(10202840887039047643)
XLA Ops:
  0.6 1.3 %multiply_convert_fusion.u_ref = bf16[128,2048]{1,0:T(8,128)(2,1)S(1)} fusion(bf16[128,2048]{1,0:T(8,128)(2,1)} %param.13, bf16[128,2048]{1,0:T(8,128)(2,1)} %param.12), kind=kLoop, calls=%fused_computation | loop fusion | flops 1048576 | bytes 1572864 | tf_op jit(solution)/shard_map/convert_element_type | solution.py:213
  2.0 4.9 %collective-permute-start = (bf16[128,2048]{1,0:T(8,128)(2,1)S(1)}, bf16[128,2048]{1,0:T(8,128)(2,1)S(1)}, u32[]{:S(2)}, u32[]{:S(2)}) collective-permute-start(bf16[128,2048]{1,0:T(8,128)(2,1)S(1)} %multiply_convert_fusion.u_ref), channel_id=1, source_target_pairs={{0,4},{4,8},{8,12},{12,16},{16,20},{20,24},{24,28},{1,5},{5,9},{9,... | collective-permute-start | bytes 1572872 | tf_op jit(solution)/shard_map/ppermute | solution.py:17
  6.9 1.3 %reshape.30.gain_ref = bf16[1,2048]{1,0:T(2,128)(2,1)} reshape(bf16[2048]{0:T(1024)(128)(2,1)} %param.15) | data formatting | bytes 8192 | tf_op jit(solution)/shard_map/reshape | solution.py:254
  8.2 1.3 %exponential_select_fusion = (f32[16,128]{1,0:T(8,128)S(1)}, f32[16,128]{1,0:T(8,128)S(1)}, f32[16,128]{1,0:T(8,128)S(1)}, f32[16,128]{1,0:T(8,128)S(1)}, f32[16...) fusion(f32[]{:T(128)S(6)} %convert_element_type.39, pred[]{:T(512)S(6)} %ne.11, ...), kind=kLoop, calls=%fused_computation.3 | loop fusion | flops 32768 | bytes 81931 | tf_op jit(solution)/shard_map/jit(_where)/select_n | solution.py:239
  9.5 14.4 %shard_map.113 = (f32[128,2048]{1,0:T(8,128)}, bf16[16,512,256]{2,1,0:T(8,128)(2,1)}, bf16[16,512,256]{2,1,0:T(8,128)(2,1)}, f32[16,64,256]{2,1,0:T(8,128)}, bf16[16,128,128]{2,1,0:T(8,128)(2,1)}) custom-call(bf16[128,2048]{1,0:T(8,128)(2,1)} %copy-done.1, bf16[128,128]{1,0:T(8,128)(2,1)} %taps_ref.1, f32[16,128]{1,0:T(8,128)} %rate_ref.1, ...), custom_call_target="tpu_custom_call" | custom-call | flops 2147483648 | bytes 573440 | tf_op jit(solution)/shard_map/pallas_call | solution.py:189
  24.0 0.8 %copy-done = bf16[128,2048]{1,0:T(8,128)(2,1)} copy-done((bf16[128,2048]{1,0:T(8,128)(2,1)}, bf16[128,2048]{1,0:T(8,128)(2,1)S(1)}, u32[]{:S(2)}) %copy-start) | copy-done | bytes 524312
  24.8 8.7 %shard_map.114 = (bf16[128,2048]{1,0:T(8,128)(2,1)}, f32[128,2048]{1,0:T(8,128)}, bf16[16,256,128]{2,1,0:T(8,128)(2,1)}, f32[1,128]{1,0:T(1,128)}) custom-call(bf16[128,2048]{1,0:T(8,128)(2,1)} %copy-done, f32[128,2048]{1,0:T(8,128)} %get-tuple-element.13.acc_ref, bf16[16,512,256]{2,1,0:T(8,128)(2,1)} %get-tuple-element.14.upper_ref, ...), custom_call_target="tpu_custom_call" | custom-call | flops 536870912 | bytes 7344128 | tf_op jit(solution)/shard_map/pallas_call | solution.py:189
  33.5 1.5 %collective-permute-start.2 = (f32[1,128]{1,0:T(1,128)}, f32[1,128]{1,0:T(1,128)S(1)}, u32[]{:S(2)}, u32[]{:S(2)}) collective-permute-start(f32[1,128]{1,0:T(1,128)} %get-tuple-element.16.refs_0_), channel_id=1, source_target_pairs={{0,2},{1,3},{2,0},{3,1},{4,6},{5,7},{6,4},{7,5},{8,10},{9,11},{10,... | collective-permute-start | bytes 1544 | tf_op jit(solution)/shard_map/ppermute | solution.py:22
  35.0 0.3 collective-permute-start.3
  35.4 1.9 %collective-permute-done.2.refs_2_ = f32[1,128]{1,0:T(1,128)S(1)} collective-permute-done((f32[1,128]{1,0:T(1,128)}, f32[1,128]{1,0:T(1,128)S(1)}, u32[]{:S(2)}, u32[]{:S(2)}) %collective-permute-start.2) | collective-permute-done | bytes 544 | tf_op jit(solution)/shard_map/ppermute | solution.py:22
  37.3 0.8 %collective-permute-done.3.refs_3_ = f32[1,128]{1,0:T(1,128)S(1)} collective-permute-done((f32[1,128]{1,0:T(1,128)}, f32[1,128]{1,0:T(1,128)S(1)}, u32[]{:S(2)}, u32[]{:S(2)}) %collective-permute-start.3) | collective-permute-done | bytes 544 | tf_op jit(solution)/shard_map/ppermute | solution.py:22
  38.1 0.5 copy-done.8
  38.6 4.5 %shard_map.115 = (f32[16,2048]{1,0:T(8,128)}, f32[1,128]{1,0:T(1,128)}) custom-call(f32[1,128]{1,0:T(1,128)} %get-tuple-element.16.refs_0_, f32[1,128]{1,0:T(1,128)} %copy-done.6, f32[1,128]{1,0:T(1,128)} %copy-done.7, f32[1,128]{1,0:T(1,128)} %copy-done.8, f32[16,64,256]{2,1,0:T(8,128)} %get-tuple-element.17.refs_4_, ...), custom_call_target="tpu_custom_call" | custom-call | flops 67108864 | bytes 2099200 | tf_op jit(solution)/shard_map/pallas_call | solution.py:189
  43.1 1.0 %convert_element_type.33 = bf16[16,2048]{1,0:T(8,128)(2,1)S(1)} convert(f32[16,2048]{1,0:T(8,128)} %get-tuple-element.19) | non-fusion elementwise | flops 32768 | bytes 196608 | tf_op jit(solution)/shard_map/convert_element_type | solution.py:273
  44.0 1.5 %collective-permute-start.4 = (bf16[16,2048]{1,0:T(8,128)(2,1)S(1)}, bf16[16,2048]{1,0:T(8,128)(2,1)S(1)}, u32[]{:S(2)}, u32[]{:S(2)}) collective-permute-start(bf16[16,2048]{1,0:T(8,128)(2,1)S(1)} %convert_element_type.33), channel_id=1, source_target_pairs={{0,4},{4,0},{8,12},{12,8},{16,20},{20,16},{24,28},{28,24},{1,5},{5... | collective-permute-start | bytes 196616 | tf_op jit(solution)/shard_map/ppermute | solution.py:22
  45.9 0.6 select_n.50
  46.5 0.3 broadcast_in_dim.28
  46.9 0.6 select_n.52
  47.5 0.9 %collective-permute-done.4.refs_0_ = bf16[16,2048]{1,0:T(8,128)(2,1)S(1)} collective-permute-done((bf16[16,2048]{1,0:T(8,128)(2,1)S(1)}, bf16[16,2048]{1,0:T(8,128)(2,1)S(1)}, u32[]{:S(2)}, u32[]{:S(2)}) %collective-permute-start.4) | collective-permute-done | bytes 65568 | tf_op jit(solution)/shard_map/ppermute | solution.py:22
  48.5 1.6 %collective-permute-start.5 = (bf16[16,2048]{1,0:T(8,128)(2,1)S(1)}, bf16[16,2048]{1,0:T(8,128)(2,1)S(1)}, u32[]{:S(2)}, u32[]{:S(2)}) collective-permute-start(bf16[16,2048]{1,0:T(8,128)(2,1)S(1)} %get-tuple-element.24), channel_id=1, source_target_pairs={{0,8},{4,12},{8,0},{12,4},{16,24},{20,28},{24,16},{28,20},{1,9},{5... | collective-permute-start | bytes 196616 | tf_op jit(solution)/shard_map/ppermute | solution.py:22
  50.1 0.3 broadcast.44
  50.4 0.6 reshape.33
  51.0 0.3 broadcast.58
  51.4 0.6 reshape.36
  52.0 0.8 %collective-permute-done.5.refs_1_ = bf16[16,2048]{1,0:T(8,128)(2,1)S(1)} collective-permute-done((bf16[16,2048]{1,0:T(8,128)(2,1)S(1)}, bf16[16,2048]{1,0:T(8,128)(2,1)S(1)}, u32[]{:S(2)}, u32[]{:S(2)}) %collective-permute-start.5) | collective-permute-done | bytes 65568 | tf_op jit(solution)/shard_map/ppermute | solution.py:22
  52.8 2.6 %collective-permute-start.6 = (bf16[16,2048]{1,0:T(8,128)(2,1)S(1)}, bf16[16,2048]{1,0:T(8,128)(2,1)S(1)}, u32[]{:S(2)}, u32[]{:S(2)}) collective-permute-start(bf16[16,2048]{1,0:T(8,128)(2,1)S(1)} %add_convert_fusion), channel_id=1, source_target_pairs={{0,16},{4,20},{8,24},{12,28},{16,0},{20,4},{24,8},{28,12},{1,17},{... | collective-permute-start | bytes 196616 | tf_op jit(solution)/shard_map/ppermute | solution.py:22
  55.8 1.3 %reshape.39.refs_3_ = f32[16,2048]{1,0:T(8,128)} reshape(f32[16,128,16]{2,1,0:T(8,128)S(1)} %broadcast.61) | data formatting | bytes 262144 | tf_op jit(solution)/shard_map/jit(_where)/select_n | solution.py:239
  57.4 1.3 %reshape.42.refs_4_ = f32[16,2048]{1,0:T(8,128)} reshape(f32[16,128,16]{2,1,0:T(8,128)S(1)} %broadcast.64) | data formatting | bytes 262144 | tf_op jit(solution)/shard_map/jit(_where)/select_n | solution.py:239
  59.0 1.3 %reshape.45.refs_5_ = f32[16,2048]{1,0:T(8,128)} reshape(f32[16,128,16]{2,1,0:T(8,128)S(1)} %broadcast.67) | data formatting | bytes 262144 | tf_op jit(solution)/shard_map/jit(_where)/select_n | solution.py:239
  60.3 7.5 %shard_map.116.refs_7_ = f32[128,2048]{1,0:T(8,128)} custom-call(f32[1,128]{1,0:T(1,128)} %get-tuple-element.21.scale_ref, f32[128,2048]{1,0:T(8,128)} %get-tuple-element.22.z_ref, bf16[16,512,256]{2,1,0:T(8,128)(2,1)} %get-tuple-element.23.square_ref), custom_call_target="tpu_custom_call" | custom-call | flops 536870912 | bytes 5243392 | tf_op jit(solution)/shard_map/pallas_call | solution.py:189
  67.9 0.6 copy-done.5
  68.5 5.0 %shard_map.117 = bf16[128,2048]{1,0:T(8,128)(2,1)} custom-call(bf16[16,2048]{1,0:T(8,128)(2,1)} %copy-done.3, bf16[16,2048]{1,0:T(8,128)(2,1)} %copy-done.4, bf16[16,2048]{1,0:T(8,128)(2,1)} %copy-done.5, f32[16,2048]{1,0:T(8,128)} %reshape.39.refs_3_, f32[16,2048]{1,0:T(8,128)} %reshape.42.refs_4_, f32[16,2048]{1,0:T(8,128)} %reshape.45.refs_5_, ...), custom_call_target="tpu_custom_call" | custom-call | flops 67108864 | bytes 2686976 | tf_op jit(solution)/shard_map/pallas_call | solution.py:189
  (25 shorter events, 1.4 us)
Async XLA Ops:
  2.0 7.6 %copy-start.1 = (bf16[128,2048]{1,0:T(8,128)(2,1)}, bf16[128,2048]{1,0:T(8,128)(2,1)S(1)}, u32[]{:S(2)}) copy-start(bf16[128,2048]{1,0:T(8,128)(2,1)S(1)} %multiply_convert_fusion.u_ref) | copy-start | bytes 1572868
  2.0 22.0 %collective-permute-start = (bf16[128,2048]{1,0:T(8,128)(2,1)S(1)}, bf16[128,2048]{1,0:T(8,128)(2,1)S(1)}, u32[]{:S(2)}, u32[]{:S(2)}) collective-permute-start(bf16[128,2048]{1,0:T(8,128)(2,1)S(1)} %multiply_convert_fusion.u_ref), channel_id=1, source_target_pairs={{0,4},{4,8},{8,12},{12,16},{16,20},{20,24},{24,28},{1,5},{5,9},{9,... | collective-permute-start | bytes 1572872 | tf_op jit(solution)/shard_map/ppermute | solution.py:17
  24.0 0.8 %copy-start = (bf16[128,2048]{1,0:T(8,128)(2,1)}, bf16[128,2048]{1,0:T(8,128)(2,1)S(1)}, u32[]{:S(2)}) copy-start(bf16[128,2048]{1,0:T(8,128)(2,1)S(1)} %collective-permute-done.halo_ref) | copy-start | bytes 1572868
  33.5 1.9 %collective-permute-start.1 = (f32[1,128]{1,0:T(1,128)}, f32[1,128]{1,0:T(1,128)S(1)}, u32[]{:S(2)}, u32[]{:S(2)}) collective-permute-start(f32[1,128]{1,0:T(1,128)} %get-tuple-element.16.refs_0_), channel_id=1, source_target_pairs={{0,1},{1,0},{2,3},{3,2},{4,5},{5,4},{6,7},{7,6},{8,9},{9,8},{10,11... | collective-permute-start | bytes 1544 | tf_op jit(solution)/shard_map/ppermute | solution.py:22
  33.5 3.8 %collective-permute-start.2 = (f32[1,128]{1,0:T(1,128)}, f32[1,128]{1,0:T(1,128)S(1)}, u32[]{:S(2)}, u32[]{:S(2)}) collective-permute-start(f32[1,128]{1,0:T(1,128)} %get-tuple-element.16.refs_0_), channel_id=1, source_target_pairs={{0,2},{1,3},{2,0},{3,1},{4,6},{5,7},{6,4},{7,5},{8,10},{9,11},{10,... | collective-permute-start | bytes 1544 | tf_op jit(solution)/shard_map/ppermute | solution.py:22
  35.0 3.1 %collective-permute-start.3 = (f32[1,128]{1,0:T(1,128)}, f32[1,128]{1,0:T(1,128)S(1)}, u32[]{:S(2)}, u32[]{:S(2)}) collective-permute-start(f32[1,128]{1,0:T(1,128)} %get-tuple-element.16.refs_0_), channel_id=1, source_target_pairs={{0,3},{1,2},{2,1},{3,0},{4,7},{5,6},{6,5},{7,4},{8,11},{9,10},{10,... | collective-permute-start | bytes 1544 | tf_op jit(solution)/shard_map/ppermute | solution.py:22
  35.4 2.7 %copy-start.6 = (f32[1,128]{1,0:T(1,128)}, f32[1,128]{1,0:T(1,128)S(1)}, u32[]{:S(2)}) copy-start(f32[1,128]{1,0:T(1,128)S(1)} %collective-permute-done.1.refs_1_) | copy-start | bytes 1540
  37.3 0.8 %copy-start.7 = (f32[1,128]{1,0:T(1,128)}, f32[1,128]{1,0:T(1,128)S(1)}, u32[]{:S(2)}) copy-start(f32[1,128]{1,0:T(1,128)S(1)} %collective-permute-done.2.refs_2_) | copy-start | bytes 1540
  38.1 0.5 copy-start.8
  43.1 5.4 %copy-start.2 = (f32[16,2048]{1,0:T(8,128)S(1)}, f32[16,2048]{1,0:T(8,128)}, u32[]{:S(2)}) copy-start(f32[16,2048]{1,0:T(8,128)} %get-tuple-element.19) | copy-start | bytes 393220
  44.0 4.4 %collective-permute-start.4 = (bf16[16,2048]{1,0:T(8,128)(2,1)S(1)}, bf16[16,2048]{1,0:T(8,128)(2,1)S(1)}, u32[]{:S(2)}, u32[]{:S(2)}) collective-permute-start(bf16[16,2048]{1,0:T(8,128)(2,1)S(1)} %convert_element_type.33), channel_id=1, source_target_pairs={{0,4},{4,0},{8,12},{12,8},{16,20},{20,16},{24,28},{28,24},{1,5},{5... | collective-permute-start | bytes 196616 | tf_op jit(solution)/shard_map/ppermute | solution.py:22
  48.4 9.0 %copy-start.3 = (bf16[16,2048]{1,0:T(8,128)(2,1)}, bf16[16,2048]{1,0:T(8,128)(2,1)S(1)}, u32[]{:S(2)}) copy-start(bf16[16,2048]{1,0:T(8,128)(2,1)S(1)} %collective-permute-done.4.refs_0_) | copy-start | bytes 196612
  48.5 4.3 %collective-permute-start.5 = (bf16[16,2048]{1,0:T(8,128)(2,1)S(1)}, bf16[16,2048]{1,0:T(8,128)(2,1)S(1)}, u32[]{:S(2)}, u32[]{:S(2)}) collective-permute-start(bf16[16,2048]{1,0:T(8,128)(2,1)S(1)} %get-tuple-element.24), channel_id=1, source_target_pairs={{0,8},{4,12},{8,0},{12,4},{16,24},{20,28},{24,16},{28,20},{1,9},{5... | collective-permute-start | bytes 196616 | tf_op jit(solution)/shard_map/ppermute | solution.py:22
  52.8 15.1 %copy-start.4 = (bf16[16,2048]{1,0:T(8,128)(2,1)}, bf16[16,2048]{1,0:T(8,128)(2,1)S(1)}, u32[]{:S(2)}) copy-start(bf16[16,2048]{1,0:T(8,128)(2,1)S(1)} %collective-permute-done.5.refs_1_) | copy-start | bytes 196612
  52.8 15.0 %collective-permute-start.6 = (bf16[16,2048]{1,0:T(8,128)(2,1)S(1)}, bf16[16,2048]{1,0:T(8,128)(2,1)S(1)}, u32[]{:S(2)}, u32[]{:S(2)}) collective-permute-start(bf16[16,2048]{1,0:T(8,128)(2,1)S(1)} %add_convert_fusion), channel_id=1, source_target_pairs={{0,16},{4,20},{8,24},{12,28},{16,0},{20,4},{24,8},{28,12},{1,17},{... | collective-permute-start | bytes 196616 | tf_op jit(solution)/shard_map/ppermute | solution.py:22
  67.8 0.6 copy-start.5

commit v2 on v1

v2 whole, which is shorter than its diff:
```python
import functools

import jax
import jax.numpy as jnp
from jax import lax
from jax.experimental import pallas as pl
from jax.experimental.pallas import tpu as pltpu
from jax.sharding import PartitionSpec as P

LANES = 128
GRANT = 16 << 20
F32, BF16 = jnp.float32, jnp.bfloat16
VMEM = pl.BlockSpec(memory_space=pltpu.VMEM)
SMEM = pl.BlockSpec(memory_space=pltpu.SMEM)
HBM = pl.BlockSpec(memory_space=pltpu.HBM)
PARTS = 4
SPAN = 16


def shifted(x, axis, by):
    peers = lax.axis_size(axis)
    return lax.ppermute(x, axis, [(i, i + by) for i in range(peers) if i + by < peers])


def swapped(x, axis, bit):
    peers = lax.axis_size(axis)
    return lax.ppermute(x, axis, [(i, i ^ bit) for i in range(peers) if i ^ bit < peers])


def everyone(x, axis):
    peers = lax.axis_size(axis)
    if peers & (peers - 1) == 0:
        return [x] + [swapped(x, axis, bit) for bit in range(1, peers)]
    turns = [[(i, (i + by) % peers) for i in range(peers)] for by in range(1, peers)]
    return [x] + [lax.ppermute(x, axis, turn) for turn in turns]


def lane_group(shape, width):
    return lax.broadcasted_iota(jnp.int32, shape, 1) // width


def by_parity(x, group_size):
    odd = jnp.where(lane_group((1, LANES), group_size) % 2 == 1, 1.0, 0.0)
    return jnp.concatenate([x * (1.0 - odd).astype(x.dtype), x * odd.astype(x.dtype)], axis=0)


def own_lanes(stacked, group_size):
    pairs = LANES // (2 * group_size)
    rows = stacked.shape[0] // pairs
    pair_of = lane_group((rows, LANES), 2 * group_size)
    out = stacked[:rows]
    for pair in range(1, pairs):
        out = jnp.where(pair_of == pair, stacked[pair * rows : (pair + 1) * rows], out)
    return out


def matmul(a, b):
    return jnp.dot(a, b, preferred_element_type=F32)


def pair_product(x, table, group_size):
    out = matmul(x, table)
    tok = out.shape[1] // 2
    return jnp.concatenate([out[:group_size, :tok], out[group_size:, tok:]], axis=0)


def turned(row, size):
    ring = pltpu.roll(jnp.broadcast_to(row, (size, size)), 0, 1, stride=1, stride_axis=0)
    return ring.astype(BF16)


def tile_of(i):
    return pl.ds(pl.multiple_of(i * LANES, LANES), LANES)


def spans(channels):
    size = max(LANES, channels // PARTS)
    return [pl.ds(start, size) for start in range(0, channels, size)]


def gate_kernel(k_hbm, v_hbm, out_ref, k_ref, v_ref, k_sem, v_sem):
    parts = spans(k_ref.shape[1])
    copies = []
    for n, at in enumerate(parts):
        copies.append(pltpu.make_async_copy(k_hbm.at[:, at], k_ref.at[:, at], k_sem.at[n]))
        copies.append(pltpu.make_async_copy(v_hbm.at[:, at], v_ref.at[:, at], v_sem.at[n]))
    for copy in copies:
        copy.start()
    for n, part in enumerate(parts):
        copies[2 * n].wait()
        copies[2 * n + 1].wait()
        for start in range(part.start, part.start + part.size, LANES):
            at = pl.ds(start, LANES)
            u = (k_ref[:, at].astype(F32) * v_ref[:, at].astype(F32)).astype(BF16)
            out_ref[at, :] = u.T


def prep_kernel(
    group_size, bits, place_ref, u_ref, weight_ref, gain_hbm, taps_hbm, rate_hbm, resid_hbm, q_hbm, k_hbm,
    base_ref, gate_ref, key_ref, upper_ref, square_ref, leave_ref, entry_ref, factor_ref, keep_ref, take_ref,
    taps, impulse, rates, weights, lower_ref, gain_ref, taps_ref, rate_ref, resid_ref, q_ref, k_ref, sems,
):
    channels, tok = u_ref.shape
    poles, groups = rate_ref.shape
    per, width = LANES // group_size, 2 * group_size
    sources = (taps_hbm, rate_hbm, gain_hbm, resid_hbm, q_hbm, k_hbm)
    places = (taps_ref, rate_ref, gain_ref, resid_ref, q_ref, k_ref)
    copies = [pltpu.make_async_copy(a, b, sems.at[n]) for n, (a, b) in enumerate(zip(sources, places))]
    for copy in copies:
        copy.start()
    row = lax.broadcasted_iota(jnp.int32, (tok, tok), 0)
    col = lax.broadcasted_iota(jnp.int32, (tok, tok), 1)
    causal = jnp.where(row <= col, 1.0, 0.0).astype(BF16)
    future = jnp.where(row <= col, 0.0, 1.0).astype(BF16)

    copies[0].wait()
    taps[...] = taps_ref[...].astype(F32)

    def taps_tables(i, _):
        for k in range(SPAN):
            ring = turned(taps[pl.ds(i * SPAN + k, 1), :], tok)
            at, cols = i * (SPAN // 2) + k // 2, pl.ds(k % 2 * tok, tok)
            lower_ref[at, :, cols] = ring * causal
            upper_ref[at, :, cols] = ring * future
        return 0

    lax.fori_loop(0, groups // SPAN, taps_tables, 0)

    copies[1].wait()
    for g in range(groups):
        at = pl.ds(g * poles, poles)
        rates[at, :] = jnp.broadcast_to(rate_ref[:, g : g + 1], (poles, tok))
        weights[at, :] = jnp.broadcast_to(weight_ref[:, g : g + 1], (poles, tok))

    position = lax.broadcasted_iota(jnp.int32, (poles, tok), 1)
    now = position.astype(F32)
    ahead = (position + 1).astype(F32)
    remain = (tok - 1 - position).astype(F32)
    place = place_ref[0]
    lane_of = lane_group((poles, LANES), group_size)

    def decays(i, _):
        spread = jnp.zeros((poles, LANES), F32)
        for k in range(per):
            at = pl.ds(pl.multiple_of((i * per + k) * poles, poles), poles)
            rate, weight = rates[at, :], weights[at, :]
            impulse[pl.ds(i * per + k, 1), :] = jnp.sum(weight * jnp.exp(-rate * now), axis=0, keepdims=True)
            leave_ref[i, pl.ds(k // 2 * poles, poles), pl.ds(k % 2 * tok, tok)] = jnp.exp(-rate * remain)
            weights[at, :] = weight * jnp.exp(-rate * ahead)
            spread = jnp.where(lane_of == k, rate, spread)
        spread = spread * tok
        at = tile_of(i)
        for step, bit in enumerate(bits):
            late = (place & bit) != 0
            behind = (place & (bit - 1)).astype(F32)
            whole = jnp.exp(-spread * bit)
            factor_ref[step, :, at] = jnp.where(late, jnp.exp(-spread * behind), 0.0)
            keep_ref[step, :, at] = jnp.where(late, 1.0, whole)
            take_ref[step, :, at] = jnp.where(late, whole, 1.0)
        return 0

    lax.fori_loop(0, channels // LANES, decays, 0, unroll=2)

    def square_tables(i, _):
        for k in range(SPAN):
            ring = turned(impulse[pl.ds(i * SPAN + k, 1), :], tok)
            square_ref[i * (SPAN // 2) + k // 2, :, pl.ds(k % 2 * tok, tok)] = ring * causal
        return 0

    lax.fori_loop(0, groups // SPAN, square_tables, 0)

    for pair in range(channels // width):
        at = pl.ds(pair * width, width)
        base_ref[at, :] = pair_product(u_ref[at, :], lower_ref[pair], group_size)

    for copy in copies[2:]:
        copy.wait()
    for i in range(channels // LANES):
        at = pl.ds(i * LANES, LANES)
        gate = q_ref[:, at].T.astype(F32)
        gate_ref[at, :] = gate
        base_ref[at, :] = resid_ref[:, at].T.astype(F32) + gate * base_ref[at, :]
        key_ref[at, :] = (k_ref[:, at].astype(F32) * gain_ref[i : i + 1, :].astype(F32)).T
        entry = weights[pl.ds(i * per * poles, per * poles), :].T
        high = entry.astype(BF16)
        entry_ref[i, :, :LANES] = high
        entry_ref[i, :, LANES:] = (entry - high.astype(F32)).astype(BF16)


def mix_kernel(group_size, halo_ref, upper_ref, base_ref, gate_ref, key_ref, mixed_ref, z_ref, sum_ref):
    channels, tok = halo_ref.shape
    width = 2 * group_size
    total = jnp.zeros((width, tok), F32)
    for pair in range(channels // width):
        at = pl.ds(pair * width, width)
        past = pair_product(halo_ref[at, :], upper_ref[pair], group_size)
        mixed = (base_ref[at, :] + gate_ref[at, :] * past).astype(BF16)
        mixed_ref[at, :] = mixed
        mixed = mixed.astype(F32)
        z_ref[at, :] = key_ref[at, :] * mixed
        total = total + mixed * mixed
    sum_ref[...] = jnp.sum(total, axis=0, keepdims=True)


def turn_kernel(group_size, z_ref, zb_ref):
    for i in range(z_ref.shape[0] // LANES):
        zb_ref[i] = by_parity(z_ref[pl.ds(i * LANES, LANES), :].astype(BF16).T, group_size)


def written(tile, out_hbm, out_ref, sem):
    copies = []
    for n, part in enumerate(spans(out_ref.shape[1])):
        for start in range(part.start, part.start + part.size, LANES):
            out_ref[:, pl.ds(start, LANES)] = tile(start // LANES)
        copies.append(pltpu.make_async_copy(out_ref.at[:, part], out_hbm.at[:, part], sem.at[n]))
        copies[-1].start()
    for copy in copies:
        copy.wait()


def out_kernel(mixed_ref, out_hbm, out_ref, sem):
    written(lambda i: mixed_ref[pl.ds(i * LANES, LANES), :].T, out_hbm, out_ref, sem)


def state_kernel(group_size, width, parts, *refs):
    sums, (leave_ref, zb_ref, state_ref, sent_ref, scale_ref) = refs[:parts], refs[parts:]
    square_sum = sums[0][...]
    for other in sums[1:]:
        square_sum = square_sum + other[...]
    scale = lax.rsqrt(square_sum / width + 1e-06)
    scale_ref[...] = scale
    twice = jnp.concatenate([scale, scale], axis=1)
    for i in range(leave_ref.shape[0]):
        at = pl.ds(i * LANES, LANES)
        leaving = (leave_ref[i] * twice).astype(BF16)
        state = own_lanes(matmul(leaving, zb_ref[i]), group_size)
        state_ref[:, at] = state
        sent_ref[:, at] = state.astype(BF16)


def local_kernel(group_size, scale_ref, z_ref, square_ref, local_ref):
    channels, tok = z_ref.shape
    width = 2 * group_size
    scale = scale_ref[...]

    def body(i, _):
        rows = []
        for pair in range(LANES // width):
            at = pl.ds(pl.multiple_of(i * LANES + pair * width, width), width)
            y = (z_ref[at, :] * scale).astype(BF16)
            rows.append(pair_product(y, square_ref[i * (LANES // width) + pair], group_size))
        local_ref[:, tile_of(i)] = jnp.concatenate(rows, axis=0).T
        return 0

    lax.fori_loop(0, channels // LANES, body, 0, unroll=4)


def final_kernel(group_size, rounds, *refs):
    got, (factor_ref, entry_ref, local_ref, q_ref, out_hbm, out_ref, sem) = refs[:rounds], refs[rounds:]
    poles, channels = got[0].shape
    per = LANES // group_size
    group_of = lane_group((poles, LANES), group_size)

    def tile(i):
        at = pl.ds(i * LANES, LANES)
        carried = factor_ref[0, :, at] * got[0][:, at].astype(F32)
        for step in range(1, rounds):
            carried = carried + factor_ref[step, :, at] * got[step][:, at].astype(F32)
        spread = [jnp.where(group_of == g, carried, 0.0).astype(BF16) for g in range(per)]
        conv = local_ref[:, at] + matmul(entry_ref[i], jnp.concatenate(spread * 2, axis=0))
        return (q_ref[:, at].astype(F32) * conv).astype(BF16)

    written(tile, out_hbm, out_ref, sem)


def held(shape, dtype):
    return jax.ShapeDtypeStruct(shape, dtype)


def call(kernel, outs, scratch, flops, *args, **more):
    size = sum(a.size * a.dtype.itemsize for a in args)
    places = more.get("in_specs", [VMEM] * len(args))
    args = [pltpu.with_memory_space_constraint(a, pltpu.HBM) if s is HBM else a for a, s in zip(args, places)]
    options = dict(
        in_specs=[VMEM] * len(args), out_specs=jax.tree.map(lambda _: VMEM, outs), scratch_shapes=scratch
    )
    return pl.pallas_call(
        kernel,
        out_shape=outs,
        cost_estimate=pl.CostEstimate(flops=flops, bytes_accessed=size, transcendentals=0),
        compiler_params=pltpu.CompilerParams(vmem_limit_bytes=GRANT),
        **{**options, **more},
    )(*args)


def per_device(resid, q_mr, k_mr, v_mr, mr_taps, norm_gain, q_lr, k_lr, pole_rate, residue):
    tok, channels = resid.shape
    groups, tap_count = mr_taps.shape
    poles = pole_rate.shape[0]
    group_size = channels // groups
    assert tap_count == tok and channels % LANES == 0 and LANES % (2 * group_size) == 0
    tiles, per = channels // LANES, LANES // group_size
    shards = lax.axis_size("ctx")
    bits = [1 << b for b in range((shards - 1).bit_length())]
    rounds = len(bits)
    place = lax.axis_index("ctx").astype(jnp.int32).reshape(1)
    work = 4 * tok * tok * channels

    rows = pltpu.VMEM((tok, channels), BF16)
    sem = pltpu.SemaphoreType.DMA((PARTS,))
    u = call(
        gate_kernel, held((channels, tok), BF16), [rows, rows, sem, sem], work // 8, k_mr, v_mr,
        in_specs=[HBM, HBM],
    )
    halo = shifted(u, "ctx", 1)

    weights = residue * jnp.sqrt(-jnp.expm1(-2.0 * pole_rate))
    tall = held((channels, tok), F32)
    table = held((groups // 2, tok, 2 * tok), BF16)
    steps = held((rounds, poles, channels), F32)
    base, gate, key, upper, square, leave, entry, factor, keep, take = call(
        functools.partial(prep_kernel, group_size, bits),
        (
            tall, tall, tall, table, table,
            held((tiles, per // 2 * poles, 2 * tok), F32),
            held((tiles, tok, 2 * per * poles), BF16),
            steps, steps, steps,
        ),
        [
            pltpu.VMEM((groups, tok), F32), pltpu.VMEM((groups, tok), F32), pltpu.VMEM((groups * poles, tok), F32),
            pltpu.VMEM((groups * poles, tok), F32), pltpu.VMEM(table.shape, BF16), pltpu.VMEM((tiles, LANES), BF16),
            pltpu.VMEM((groups, tok), BF16), pltpu.VMEM((poles, groups), F32), rows, rows, rows,
            pltpu.SemaphoreType.DMA((6,)),
        ],
        8 * work,
        place, u, weights, norm_gain.reshape(tiles, LANES), mr_taps, pole_rate, resid, q_mr, k_lr,
        in_specs=[SMEM, VMEM, VMEM] + [HBM] * 6,
    )
    mixed_t, z, square_sum = call(
        functools.partial(mix_kernel, group_size),
        (held((channels, tok), BF16), tall, held((1, tok), F32)),
        [],
        work,
        halo, upper, base, gate, key,
    )
    sums = everyone(square_sum, "tp")
    zb = call(
        functools.partial(turn_kernel, group_size), held((tiles, 2 * tok, LANES), BF16), [], work // 2, z
    )
    small = (poles, channels)
    state, sent, scale = call(
        functools.partial(state_kernel, group_size, channels * lax.axis_size("tp"), len(sums)),
        (held(small, F32), held(small, BF16), held((1, tok), F32)),
        [],
        work // 8,
        *sums, leave, zb,
    )
    local = call(
        functools.partial(local_kernel, group_size),
        held((tok, channels), F32),
        [],
        work,
        scale, z, square,
    )
    got = []
    for step, bit in enumerate(bits):
        got.append(swapped(sent, "ctx", bit))
        state = keep[step] * state + take[step] * got[step].astype(F32)
        sent = state.astype(BF16)
    mixed = call(out_kernel, held((tok, channels), BF16), [rows, sem], work // 4, mixed_t, out_specs=HBM)
    lr_out = call(
        functools.partial(final_kernel, group_size, rounds),
        held((tok, channels), BF16),
        [rows, sem],
        work // 8,
        *got, factor, entry, local, q_lr,
        out_specs=HBM,
    )
    return (mixed, lr_out)


def solution(mesh):
    whole, tables = P("ctx", "tp"), P(None, "tp")
    placed = (whole,) * 4 + (P("tp", None), P("tp")) + (whole,) * 2 + (tables,) * 2
    return jax.shard_map(
        per_device, mesh=mesh, in_specs=placed, out_specs=(whole, whole), check_vma=False
    )
```

time: 73.8 us -> 40.2 us (0.54)
  Pallas kernels: 40.2 us -> 14 us
  local copies, waits for them, and re-layouts: 11.9 us -> 0.01 us
  waiting for transfers between devices: 4.45 us -> 9.15 us
  other arithmetic: 3.7 us -> 0.81 us
  starting transfers between devices: 12.5 us -> 15.3 us
    pallas_call x5 -> x8, Pallas kernels: 40.2 us -> 14 us  [call(): pl.pallas_call(kernel, out_shape=outs, cost_estimate=pl.CostEstimate(flop...]
    select_n x7 -> x0, local copies, waits for them, and re-layouts: 6.38 us -> none  [the longest x3 3.87 us: per_device(): factors.append(jnp.where(late, jnp.exp(-rate * behind), 0.0))]
    ppermute x6, starting transfers between devices: 7.61 us -> 10.3 us  [swapped(): lax.ppermute(x, axis, [(i, i ^ bit) for i in range(peers) if i ^ bit < pe...]
    ppermute x1, waiting for transfers between devices: 0.01 us -> 2.65 us  [shifted(): lax.ppermute(x, axis, [(i, i + by) for i in range(peers) if i + by < peers])]
    convert_element_type x4 -> x2, other arithmetic: 2.36 us -> 0.08 us  [per_device(): sent = state.astype(BF16)]
    broadcast_in_dim x7 -> x0, local copies, waits for them, and re-layouts: 2.26 us -> none  [per_device(): rate = jnp.repeat(pole_rate, group_size, axis=1) * tok]
    ppermute x6, waiting for transfers between devices: 4.45 us -> 6.5 us  [swapped(): lax.ppermute(x, axis, [(i, i ^ bit) for i in range(peers) if i ^ bit < pe...]
    unnamed x18 -> x2, local copies, waits for them, and re-layouts: 1.92 us -> 0.01 us
  transfers between devices with their start and end apart: 7 -> 7, of which waited for: 4 -> 5; matrix products, arithmetic and copies ran while one was open for 15% -> 2% of each run, Pallas kernels for 30% -> 26%
where the time goes in v2:
time: 40.2 us; the launch traced here: 39.9 us
  starting transfers between devices  15.3 us (38%)
  Pallas kernels  14 us (35%)
  waiting for transfers between devices  9.15 us (23%)
  other arithmetic  0.81 us (2%)
  between operations  0.72 us (2%)
    pallas_call x8, Pallas kernels, call(): pl.pallas_call(kernel, out_shape=outs, cost_estimate=pl.CostEstimate(flop...  14 us
    ppermute x6, starting transfers between devices, swapped(): lax.ppermute(x, axis, [(i, i ^ bit) for i in range(peers) if i ^ bit < pe...  10.3 us
    ppermute x6, waiting for transfers between devices, swapped(): lax.ppermute(x, axis, [(i, i ^ bit) for i in range(peers) if i ^ bit < pe...  6.5 us
    ppermute x1, starting transfers between devices, shifted(): lax.ppermute(x, axis, [(i, i + by) for i in range(peers) if i + by < peers])  4.9 us
    ppermute x1, waiting for transfers between devices, shifted(): lax.ppermute(x, axis, [(i, i + by) for i in range(peers) if i + by < peers])  2.65 us
  transfers between devices with their start and end apart: 7, of which 5 were waited for; matrix products, arithmetic and copies ran while one was open for 2% of the time, Pallas kernels for 26%

profile of v2, /device:TPU:0, one launch (start us, length us, event | category | flops | bytes accessed | tf_op | source)
XLA Modules:
  0.0 39.9 jit_solution(10581621463807672847)
XLA Ops:
  0.6 1.5 %shard_map.113.u_ref = bf16[2048,128]{1,0:T(8,128)(2,1)S(1)} custom-call(bf16[128,2048]{1,0:T(8,128)(2,1)} %k_hbm.2, bf16[128,2048]{1,0:T(8,128)(2,1)} %v_hbm.1), custom_call_target="tpu_custom_call" | custom-call | flops 16777216 | bytes 1048576 | tf_op jit(solution)/shard_map/pallas_call | solution.py:287
  2.1 4.9 %collective-permute-start = (bf16[2048,128]{1,0:T(8,128)(2,1)S(1)}, bf16[2048,128]{1,0:T(8,128)(2,1)S(1)}, u32[]{:S(2)}, u32[]{:S(2)}) collective-permute-start(bf16[2048,128]{1,0:T(8,128)(2,1)S(1)} %shard_map.113.u_ref), channel_id=1, source_target_pairs={{0,4},{4,8},{8,12},{12,16},{16,20},{20,24},{24,28},{1,5},{5,9},{9,... | collective-permute-start | bytes 1572872 | tf_op jit(solution)/shard_map/ppermute | solution.py:22
  7.0 0.7 %sqrt_multiply_fusion.weight_ref = f32[16,128]{1,0:T(8,128)S(1)} fusion(f32[16,128]{1,0:T(8,128)} %param.19, f32[16,128]{1,0:T(8,128)} %rate_hbm.1), kind=kLoop, calls=%fused_computation.7 | loop fusion | flops 6144 | bytes 24576 | tf_op jit(solution)/shard_map/mul | solution.py:317
  7.8 7.7 %shard_map.114 = (f32[2048,128]{1,0:T(8,128)S(1)}, f32[2048,128]{1,0:T(8,128)S(1)}, f32[2048,128]{1,0:T(8,128)S(1)}, bf16[64,128,256]{2,1,0:T(8,128)(2,1)S(1)}, ...) custom-call(s32[1]{0:T(128)} %bitcast.place_ref, ...), custom_call_target="tpu_custom_call" | custom-call | flops 1073741824 | bytes 2150404 | tf_op jit(solution)/shard_map/pallas_call | solution.py:287
  15.5 2.6 %collective-permute-done.halo_ref = bf16[2048,128]{1,0:T(8,128)(2,1)S(1)} collective-permute-done((bf16[2048,128]{1,0:T(8,128)(2,1)S(1)}, bf16[2048,128]{1,0:T(8,128)(2,1)S(1)}, u32[]{:S(2)}, u32[]{:S(2)}) %collective-permute-start) | collective-permute-done | bytes 524320 | tf_op jit(solution)/shard_map/ppermute | solution.py:22
  18.1 0.8 %shard_map.115 = (bf16[2048,128]{1,0:T(8,128)(2,1)S(1)}, f32[2048,128]{1,0:T(8,128)S(1)}, f32[1,128]{1,0:T(1,128)S(1)}) custom-call(bf16[2048,128]{1,0:T(8,128)(2,1)S(1)} %collective-permute-done.halo_ref, bf16[64,128,256]{2,1,0:T(8,128)(2,1)S(1)} %get-tuple-element.18.upper_ref, f32[2048,128]{1,0:T(8,128)S(1)} %get-tuple-element.19.base_ref, ...), custom_call_target="tpu_custom_call" | custom-call | flops 134217728 | bytes 7864320 | tf_op jit(solution)/shard_map/pallas_call | solution.py:287
  18.9 0.2 collective-permute-start.3
  19.1 1.5 %collective-permute-start.2 = (f32[1,128]{1,0:T(1,128)S(1)}, f32[1,128]{1,0:T(1,128)S(1)}, u32[]{:S(2)}, u32[]{:S(2)}) collective-permute-start(f32[1,128]{1,0:T(1,128)S(1)} %get-tuple-element.23.refs_0_), channel_id=1, source_target_pairs={{0,2},{1,3},{2,0},{3,1},{4,6},{5,7},{6,4},{7,5},{8,10},{9,11},{10,... | collective-permute-start | bytes 1544 | tf_op jit(solution)/shard_map/ppermute | solution.py:27
  20.6 0.3 collective-permute-start.1
  20.9 0.2 shard_map.117.refs_5_
  21.1 0.9 %collective-permute-done.3.refs_3_ = f32[1,128]{1,0:T(1,128)S(1)} collective-permute-done((f32[1,128]{1,0:T(1,128)S(1)}, f32[1,128]{1,0:T(1,128)S(1)}, u32[]{:S(2)}, u32[]{:S(2)}) %collective-permute-start.3) | collective-permute-done | bytes 544 | tf_op jit(solution)/shard_map/ppermute | solution.py:27
  22.0 0.7 %collective-permute-done.2.refs_2_ = f32[1,128]{1,0:T(1,128)S(1)} collective-permute-done((f32[1,128]{1,0:T(1,128)S(1)}, f32[1,128]{1,0:T(1,128)S(1)}, u32[]{:S(2)}, u32[]{:S(2)}) %collective-permute-start.2) | collective-permute-done | bytes 544 | tf_op jit(solution)/shard_map/ppermute | solution.py:27
  22.7 0.0 collective-permute-done.1.refs_1_
  22.7 0.3 shard_map.118
  23.0 2.5 %collective-permute-start.4 = (bf16[16,2048]{1,0:T(8,128)(2,1)S(1)}, bf16[16,2048]{1,0:T(8,128)(2,1)S(1)}, u32[]{:S(2)}, u32[]{:S(2)}) collective-permute-start(bf16[16,2048]{1,0:T(8,128)(2,1)S(1)} %get-tuple-element.26), channel_id=1, source_target_pairs={{0,4},{4,0},{8,12},{12,8},{16,20},{20,16},{24,28},{28,24},{1,5},{5... | collective-permute-start | bytes 196616 | tf_op jit(solution)/shard_map/ppermute | solution.py:27
  25.6 2.6 %collective-permute-done.4.refs_0_ = bf16[16,2048]{1,0:T(8,128)(2,1)S(1)} collective-permute-done((bf16[16,2048]{1,0:T(8,128)(2,1)S(1)}, bf16[16,2048]{1,0:T(8,128)(2,1)S(1)}, u32[]{:S(2)}, u32[]{:S(2)}) %collective-permute-start.4) | collective-permute-done | bytes 65568 | tf_op jit(solution)/shard_map/ppermute | solution.py:27
  28.2 0.0 copy-start
  28.2 2.8 %collective-permute-start.5 = (bf16[16,2048]{1,0:T(8,128)(2,1)S(1)}, bf16[16,2048]{1,0:T(8,128)(2,1)S(1)}, u32[]{:S(2)}, u32[]{:S(2)}) collective-permute-start(bf16[16,2048]{1,0:T(8,128)(2,1)S(1)} %get-tuple-element.34), channel_id=1, source_target_pairs={{0,8},{4,12},{8,0},{12,4},{16,24},{20,28},{24,16},{28,20},{1,9},{5... | collective-permute-start | bytes 196616 | tf_op jit(solution)/shard_map/ppermute | solution.py:27
  31.0 2.2 %collective-permute-done.5.refs_1_ = bf16[16,2048]{1,0:T(8,128)(2,1)S(1)} collective-permute-done((bf16[16,2048]{1,0:T(8,128)(2,1)S(1)}, bf16[16,2048]{1,0:T(8,128)(2,1)S(1)}, u32[]{:S(2)}, u32[]{:S(2)}) %collective-permute-start.5) | collective-permute-done | bytes 65568 | tf_op jit(solution)/shard_map/ppermute | solution.py:27
  33.3 3.1 %collective-permute-start.6 = (bf16[16,2048]{1,0:T(8,128)(2,1)S(1)}, bf16[16,2048]{1,0:T(8,128)(2,1)S(1)}, u32[]{:S(2)}, u32[]{:S(2)}) collective-permute-start(bf16[16,2048]{1,0:T(8,128)(2,1)S(1)} %fusion.1), channel_id=1, source_target_pairs={{0,16},{4,20},{8,24},{12,28},{16,0},{20,4},{24,8},{28,12},{1,17},{... | collective-permute-start | bytes 196616 | tf_op jit(solution)/shard_map/ppermute | solution.py:27
  36.4 0.9 %shard_map.116 = bf16[128,2048]{1,0:T(8,128)(2,1)} custom-call(bf16[2048,128]{1,0:T(8,128)(2,1)S(1)} %get-tuple-element.22.mixed_ref), custom_call_target="tpu_custom_call" | custom-call | flops 33554432 | bytes 524288 | tf_op jit(solution)/shard_map/pallas_call | solution.py:287
  37.3 1.4 %shard_map.119.refs_5_ = f32[128,2048]{1,0:T(8,128)S(1)} custom-call(f32[1,128]{1,0:T(1,128)S(1)} %get-tuple-element.32.scale_ref, f32[2048,128]{1,0:T(8,128)S(1)} %get-tuple-element.25.z_ref, bf16[64,128,256]{2,1,0:T(8,128)(2,1)S(1)} %get-tuple-element.33.square_ref), custom_call_target="tpu_custom_call" | custom-call | flops 134217728 | bytes 5243392 | tf_op jit(solution)/shard_map/pallas_call | solution.py:287
  38.7 0.0 collective-permute-done.6.refs_2_
  38.7 0.0 copy-done
  38.8 1.2 %shard_map.120 = bf16[128,2048]{1,0:T(8,128)(2,1)} custom-call(bf16[16,2048]{1,0:T(8,128)(2,1)S(1)} %collective-permute-done.4.refs_0_, bf16[16,2048]{1,0:T(8,128)(2,1)S(1)} %collective-permute-done.5.refs_1_, bf16[16,2048]{1,0:T(8,128)(2,1)S(1)} %collective-permute-done.6.refs_2_, f32[3,16,2048]{2,1,0:T(8,128)S(1)} %get-tuple-element.30.refs_3_, ...), custom_call_target="tpu_custom_call" | custom-call | flops 16777216 | bytes 3211264 | tf_op jit(solution)/shard_map/pallas_call | solution.py:287
  (2 shorter events, 0.1 us)
Async XLA Ops:
  2.1 16.0 %collective-permute-start = (bf16[2048,128]{1,0:T(8,128)(2,1)S(1)}, bf16[2048,128]{1,0:T(8,128)(2,1)S(1)}, u32[]{:S(2)}, u32[]{:S(2)}) collective-permute-start(bf16[2048,128]{1,0:T(8,128)(2,1)S(1)} %shard_map.113.u_ref), channel_id=1, source_target_pairs={{0,4},{4,8},{8,12},{12,16},{16,20},{20,24},{24,28},{1,5},{5,9},{9,... | collective-permute-start | bytes 1572872 | tf_op jit(solution)/shard_map/ppermute | solution.py:22
  18.9 3.1 %collective-permute-start.3 = (f32[1,128]{1,0:T(1,128)S(1)}, f32[1,128]{1,0:T(1,128)S(1)}, u32[]{:S(2)}, u32[]{:S(2)}) collective-permute-start(f32[1,128]{1,0:T(1,128)S(1)} %get-tuple-element.23.refs_0_), channel_id=1, source_target_pairs={{0,3},{1,2},{2,1},{3,0},{4,7},{5,6},{6,5},{7,4},{8,11},{9,10},{10,... | collective-permute-start | bytes 1544 | tf_op jit(solution)/shard_map/ppermute | solution.py:27
  19.1 3.6 %collective-permute-start.2 = (f32[1,128]{1,0:T(1,128)S(1)}, f32[1,128]{1,0:T(1,128)S(1)}, u32[]{:S(2)}, u32[]{:S(2)}) collective-permute-start(f32[1,128]{1,0:T(1,128)S(1)} %get-tuple-element.23.refs_0_), channel_id=1, source_target_pairs={{0,2},{1,3},{2,0},{3,1},{4,6},{5,7},{6,4},{7,5},{8,10},{9,11},{10,... | collective-permute-start | bytes 1544 | tf_op jit(solution)/shard_map/ppermute | solution.py:27
  20.6 2.1 %collective-permute-start.1 = (f32[1,128]{1,0:T(1,128)S(1)}, f32[1,128]{1,0:T(1,128)S(1)}, u32[]{:S(2)}, u32[]{:S(2)}) collective-permute-start(f32[1,128]{1,0:T(1,128)S(1)} %get-tuple-element.23.refs_0_), channel_id=1, source_target_pairs={{0,1},{1,0},{2,3},{3,2},{4,5},{5,4},{6,7},{7,6},{8,9},{9,8},{10,11... | collective-permute-start | bytes 1544 | tf_op jit(solution)/shard_map/ppermute | solution.py:27
  23.0 5.2 %collective-permute-start.4 = (bf16[16,2048]{1,0:T(8,128)(2,1)S(1)}, bf16[16,2048]{1,0:T(8,128)(2,1)S(1)}, u32[]{:S(2)}, u32[]{:S(2)}) collective-permute-start(bf16[16,2048]{1,0:T(8,128)(2,1)S(1)} %get-tuple-element.26), channel_id=1, source_target_pairs={{0,4},{4,0},{8,12},{12,8},{16,20},{20,16},{24,28},{28,24},{1,5},{5... | collective-permute-start | bytes 196616 | tf_op jit(solution)/shard_map/ppermute | solution.py:27
  28.2 10.5 %copy-start = (bf16[128,2048]{1,0:T(8,128)(2,1)S(1)}, bf16[128,2048]{1,0:T(8,128)(2,1)}, u32[]{:S(2)}) copy-start(bf16[128,2048]{1,0:T(8,128)(2,1)} %refs_6_.1) | copy-start | bytes 1572868
  28.2 5.0 %collective-permute-start.5 = (bf16[16,2048]{1,0:T(8,128)(2,1)S(1)}, bf16[16,2048]{1,0:T(8,128)(2,1)S(1)}, u32[]{:S(2)}, u32[]{:S(2)}) collective-permute-start(bf16[16,2048]{1,0:T(8,128)(2,1)S(1)} %get-tuple-element.34), channel_id=1, source_target_pairs={{0,8},{4,12},{8,0},{12,4},{16,24},{20,28},{24,16},{28,20},{1,9},{5... | collective-permute-start | bytes 196616 | tf_op jit(solution)/shard_map/ppermute | solution.py:27
  33.3 5.4 %collective-permute-start.6 = (bf16[16,2048]{1,0:T(8,128)(2,1)S(1)}, bf16[16,2048]{1,0:T(8,128)(2,1)S(1)}, u32[]{:S(2)}, u32[]{:S(2)}) collective-permute-start(bf16[16,2048]{1,0:T(8,128)(2,1)S(1)} %fusion.1), channel_id=1, source_target_pairs={{0,16},{4,20},{8,24},{12,28},{16,0},{20,4},{24,8},{28,12},{1,17},{... | collective-permute-start | bytes 196616 | tf_op jit(solution)/shard_map/ppermute | solution.py:27

commit v3 on v2

--- a/solution.py
+++ b/solution.py
@@ -14,6 +14,8 @@
 SMEM = pl.BlockSpec(memory_space=pltpu.SMEM)
 HBM = pl.BlockSpec(memory_space=pltpu.HBM)
 PARTS = 4
+CHUNKS = 2
+SMALL, TERMS = 0.5, 10
 SPAN = 16
 
 
@@ -69,6 +71,13 @@
     return ring.astype(BF16)
 
 
+def series(x):
+    out = jnp.ones_like(x)
+    for n in range(TERMS, 1, -1):
+        out = 1.0 - x / n * out
+    return out
+
+
 def tile_of(i):
     return pl.ds(pl.multiple_of(i * LANES, LANES), LANES)
 
@@ -78,33 +87,39 @@
     return [pl.ds(start, size) for start in range(0, channels, size)]
 
 
-def gate_kernel(k_hbm, v_hbm, out_ref, k_ref, v_ref, k_sem, v_sem):
-    parts = spans(k_ref.shape[1])
+def gated(k, v, out_ref):
+    for start in range(0, out_ref.shape[0], LANES):
+        at = pl.ds(start, LANES)
+        out_ref[at, :] = (k[:, at].astype(F32) * v[:, at].astype(F32)).astype(BF16).T
+
+
+def first_kernel(k_hbm, v_hbm, out_ref, *refs):
+    later, (k_ref, v_ref, sems) = refs[:-3], refs[-3:]
+    chunk = out_ref.shape[0]
     copies = []
-    for n, at in enumerate(parts):
-        copies.append(pltpu.make_async_copy(k_hbm.at[:, at], k_ref.at[:, at], k_sem.at[n]))
-        copies.append(pltpu.make_async_copy(v_hbm.at[:, at], v_ref.at[:, at], v_sem.at[n]))
-    for copy in copies:
-        copy.start()
-    for n, part in enumerate(parts):
-        copies[2 * n].wait()
-        copies[2 * n + 1].wait()
-        for start in range(part.start, part.start + part.size, LANES):
-            at = pl.ds(start, LANES)
-            u = (k_ref[:, at].astype(F32) * v_ref[:, at].astype(F32)).astype(BF16)
-            out_ref[at, :] = u.T
+    for n, to in enumerate((k_ref, v_ref) + later):
+        source = (k_hbm, v_hbm)[n % 2].at[:, pl.ds(n // 2 * chunk, chunk)]
+        copies.append(pltpu.make_async_copy(source, to, sems.at[n]))
+        copies[-1].start()
+    copies[0].wait()
+    copies[1].wait()
+    gated(k_ref, v_ref, out_ref)
+    for copy in copies[2:]:
+        copy.wait()
 
 
 def prep_kernel(
-    group_size, bits, place_ref, u_ref, weight_ref, gain_hbm, taps_hbm, rate_hbm, resid_hbm, q_hbm, k_hbm,
+    group_size, bits, place_ref, u_refs, gain_hbm, taps_hbm, rate_hbm, residue_hbm, resid_hbm, q_hbm, k_hbm,
     base_ref, gate_ref, key_ref, upper_ref, square_ref, leave_ref, entry_ref, factor_ref, keep_ref, take_ref,
-    taps, impulse, rates, weights, lower_ref, gain_ref, taps_ref, rate_ref, resid_ref, q_ref, k_ref, sems,
+    taps, impulse, rates, weights, lower_ref,
+    gain_ref, taps_ref, rate_ref, residue_ref, resid_ref, q_ref, k_ref, sems,
 ):
-    channels, tok = u_ref.shape
+    chunk, tok = u_refs[0].shape
+    channels = chunk * len(u_refs)
     poles, groups = rate_ref.shape
     per, width = LANES // group_size, 2 * group_size
-    sources = (taps_hbm, rate_hbm, gain_hbm, resid_hbm, q_hbm, k_hbm)
-    places = (taps_ref, rate_ref, gain_ref, resid_ref, q_ref, k_ref)
+    sources = (taps_hbm, rate_hbm, residue_hbm, gain_hbm, resid_hbm, q_hbm, k_hbm)
+    places = (taps_ref, rate_ref, residue_ref, gain_ref, resid_ref, q_ref, k_ref)
     copies = [pltpu.make_async_copy(a, b, sems.at[n]) for n, (a, b) in enumerate(zip(sources, places))]
     for copy in copies:
         copy.start()
@@ -127,10 +142,13 @@
     lax.fori_loop(0, groups // SPAN, taps_tables, 0)
 
     copies[1].wait()
+    copies[2].wait()
+    twice = 2.0 * rate_ref[...]
+    weight = residue_ref[...] * jnp.sqrt(jnp.where(twice < SMALL, twice * series(twice), 1.0 - jnp.exp(-twice)))
     for g in range(groups):
         at = pl.ds(g * poles, poles)
         rates[at, :] = jnp.broadcast_to(rate_ref[:, g : g + 1], (poles, tok))
-        weights[at, :] = jnp.broadcast_to(weight_ref[:, g : g + 1], (poles, tok))
+        weights[at, :] = jnp.broadcast_to(weight[:, g : g + 1], (poles, tok))
 
     position = lax.broadcasted_iota(jnp.int32, (poles, tok), 1)
     now = position.astype(F32)
@@ -171,9 +189,10 @@
 
     for pair in range(channels // width):
         at = pl.ds(pair * width, width)
-        base_ref[at, :] = pair_product(u_ref[at, :], lower_ref[pair], group_size)
-
-    for copy in copies[2:]:
+        u = u_refs[pair * width // chunk][pl.ds(pair * width % chunk, width), :]
+        base_ref[at, :] = pair_product(u, lower_ref[pair], group_size)
+
+    for copy in copies[3:]:
         copy.wait()
     for i in range(channels // LANES):
         at = pl.ds(i * LANES, LANES)
@@ -187,24 +206,33 @@
         entry_ref[i, :, LANES:] = (entry - high.astype(F32)).astype(BF16)
 
 
-def mix_kernel(group_size, halo_ref, upper_ref, base_ref, gate_ref, key_ref, mixed_ref, z_ref, sum_ref):
+def mix_kernel(group_size, first, halo_ref, upper_ref, base_ref, gate_ref, key_ref, *refs):
+    before, (mixed_ref, z_ref, sum_ref) = refs[:-3], refs[-3:]
     channels, tok = halo_ref.shape
     width = 2 * group_size
     total = jnp.zeros((width, tok), F32)
     for pair in range(channels // width):
-        at = pl.ds(pair * width, width)
-        past = pair_product(halo_ref[at, :], upper_ref[pair], group_size)
-        mixed = (base_ref[at, :] + gate_ref[at, :] * past).astype(BF16)
+        at, there = pl.ds(pair * width, width), pl.ds(first + pair * width, width)
+        past = pair_product(halo_ref[at, :], upper_ref[first // width + pair], group_size)
+        mixed = (base_ref[there, :] + gate_ref[there, :] * past).astype(BF16)
         mixed_ref[at, :] = mixed
         mixed = mixed.astype(F32)
-        z_ref[at, :] = key_ref[at, :] * mixed
+        z_ref[at, :] = key_ref[there, :] * mixed
         total = total + mixed * mixed
-    sum_ref[...] = jnp.sum(total, axis=0, keepdims=True)
-
-
-def turn_kernel(group_size, z_ref, zb_ref):
-    for i in range(z_ref.shape[0] // LANES):
-        zb_ref[i] = by_parity(z_ref[pl.ds(i * LANES, LANES), :].astype(BF16).T, group_size)
+    total = jnp.sum(total, axis=0, keepdims=True)
+    for ref in before:
+        total = total + ref[...]
+    sum_ref[...] = total
+
+
+def rows_of(refs, start, size):
+    chunk = refs[0].shape[0]
+    return refs[start // chunk][pl.ds(start % chunk, size), :]
+
+
+def turn_kernel(group_size, z_refs, zb_ref):
+    for i in range(zb_ref.shape[0]):
+        zb_ref[i] = by_parity(rows_of(z_refs, i * LANES, LANES).astype(BF16).T, group_size)
 
 
 def written(tile, out_hbm, out_ref, sem):
@@ -218,8 +246,8 @@
         copy.wait()
 
 
-def out_kernel(mixed_ref, out_hbm, out_ref, sem):
-    written(lambda i: mixed_ref[pl.ds(i * LANES, LANES), :].T, out_hbm, out_ref, sem)
+def out_kernel(mixed_refs, out_hbm, out_ref, sem):
+    written(lambda i: rows_of(mixed_refs, i * LANES, LANES).T, out_hbm, out_ref, sem)
 
 
 def state_kernel(group_size, width, parts, *refs):
@@ -238,21 +266,23 @@
         sent_ref[:, at] = state.astype(BF16)
 
 
-def local_kernel(group_size, scale_ref, z_ref, square_ref, local_ref):
-    channels, tok = z_ref.shape
+def local_kernel(group_size, scale_ref, z_refs, square_ref, local_ref):
+    chunk = z_refs[0].shape[0]
     width = 2 * group_size
     scale = scale_ref[...]
-
-    def body(i, _):
-        rows = []
-        for pair in range(LANES // width):
-            at = pl.ds(pl.multiple_of(i * LANES + pair * width, width), width)
-            y = (z_ref[at, :] * scale).astype(BF16)
-            rows.append(pair_product(y, square_ref[i * (LANES // width) + pair], group_size))
-        local_ref[:, tile_of(i)] = jnp.concatenate(rows, axis=0).T
-        return 0
-
-    lax.fori_loop(0, channels // LANES, body, 0, unroll=4)
+    for n, z_ref in enumerate(z_refs):
+
+        def body(i, _):
+            rows = []
+            for pair in range(LANES // width):
+                at = pl.ds(pl.multiple_of(i * LANES + pair * width, width), width)
+                y = (z_ref[at, :] * scale).astype(BF16)
+                table = square_ref[n * (chunk // width) + i * (LANES // width) + pair]
+                rows.append(pair_product(y, table, group_size))
+            local_ref[:, tile_of(n * (chunk // LANES) + i)] = jnp.concatenate(rows, axis=0).T
+            return 0
+
+        lax.fori_loop(0, chunk // LANES, body, 0, unroll=4)
 
 
 def final_kernel(group_size, rounds, *refs):
@@ -278,18 +308,18 @@
 
 
 def call(kernel, outs, scratch, flops, *args, **more):
-    size = sum(a.size * a.dtype.itemsize for a in args)
     places = more.get("in_specs", [VMEM] * len(args))
     args = [pltpu.with_memory_space_constraint(a, pltpu.HBM) if s is HBM else a for a, s in zip(args, places)]
-    options = dict(
-        in_specs=[VMEM] * len(args), out_specs=jax.tree.map(lambda _: VMEM, outs), scratch_shapes=scratch
-    )
+    specs = [[s] * len(a) if isinstance(a, list) else s for a, s in zip(args, places)]
+    size = sum(a.size * a.dtype.itemsize for a in jax.tree.leaves(args))
     return pl.pallas_call(
         kernel,
+        in_specs=specs,
+        out_specs=more.get("out_specs", jax.tree.map(lambda _: VMEM, outs)),
         out_shape=outs,
+        scratch_shapes=scratch,
         cost_estimate=pl.CostEstimate(flops=flops, bytes_accessed=size, transcendentals=0),
         compiler_params=pltpu.CompilerParams(vmem_limit_bytes=GRANT),
-        **{**options, **more},
     )(*args)
 
 
@@ -306,15 +336,22 @@
     place = lax.axis_index("ctx").astype(jnp.int32).reshape(1)
     work = 4 * tok * tok * channels
 
+    chunk = channels // CHUNKS
+    firsts = range(0, channels, chunk)
+    part = pltpu.VMEM((tok, chunk), BF16)
     rows = pltpu.VMEM((tok, channels), BF16)
     sem = pltpu.SemaphoreType.DMA((PARTS,))
-    u = call(
-        gate_kernel, held((channels, tok), BF16), [rows, rows, sem, sem], work // 8, k_mr, v_mr,
-        in_specs=[HBM, HBM],
-    )
-    halo = shifted(u, "ctx", 1)
-
-    weights = residue * jnp.sqrt(-jnp.expm1(-2.0 * pole_rate))
+    late = [held((tok, chunk), BF16)] * (2 * CHUNKS - 2)
+    outs = call(
+        first_kernel, [held((chunk, tok), BF16)] + late, [part, part, pltpu.SemaphoreType.DMA((2 * CHUNKS,))],
+        work // 8, k_mr, v_mr, in_specs=[HBM, HBM],
+    )
+    u = [outs[0]]
+    halo = [shifted(u[0], "ctx", 1)]
+    for n in range(1, len(outs), 2):
+        u.append(call(gated, held((chunk, tok), BF16), [], work // 8, *outs[n : n + 2]))
+        halo.append(shifted(u[-1], "ctx", 1))
+
     tall = held((channels, tok), F32)
     table = held((groups // 2, tok, 2 * tok), BF16)
     steps = held((rounds, poles, channels), F32)
@@ -329,20 +366,26 @@
         [
             pltpu.VMEM((groups, tok), F32), pltpu.VMEM((groups, tok), F32), pltpu.VMEM((groups * poles, tok), F32),
             pltpu.VMEM((groups * poles, tok), F32), pltpu.VMEM(table.shape, BF16), pltpu.VMEM((tiles, LANES), BF16),
-            pltpu.VMEM((groups, tok), BF16), pltpu.VMEM((poles, groups), F32), rows, rows, rows,
-            pltpu.SemaphoreType.DMA((6,)),
+            pltpu.VMEM((groups, tok), BF16), pltpu.VMEM((poles, groups), F32), pltpu.VMEM((poles, groups), F32),
+            rows, rows, rows, pltpu.SemaphoreType.DMA((7,)),
         ],
         8 * work,
-        place, u, weights, norm_gain.reshape(tiles, LANES), mr_taps, pole_rate, resid, q_mr, k_lr,
-        in_specs=[SMEM, VMEM, VMEM] + [HBM] * 6,
-    )
-    mixed_t, z, square_sum = call(
-        functools.partial(mix_kernel, group_size),
-        (held((channels, tok), BF16), tall, held((1, tok), F32)),
-        [],
-        work,
-        halo, upper, base, gate, key,
-    )
+        place, u, norm_gain.reshape(tiles, LANES), mr_taps, pole_rate, residue, resid, q_mr, k_lr,
+        in_specs=[SMEM, VMEM] + [HBM] * 7,
+    )
+    mixed_t, z, square_sum = [], [], []
+    for first, past in zip(firsts, halo):
+        outs = call(
+            functools.partial(mix_kernel, group_size, first),
+            (held((chunk, tok), BF16), held((chunk, tok), F32), held((1, tok), F32)),
+            [],
+            work // CHUNKS,
+            past, upper, base, gate, key, *square_sum,
+        )
+        mixed_t.append(outs[0])
+        z.append(outs[1])
+        square_sum = [outs[2]]
+    square_sum = square_sum[0]
     sums = everyone(square_sum, "tp")
     zb = call(
         functools.partial(turn_kernel, group_size), held((tiles, 2 * tok, LANES), BF16), [], work // 2, z

time: 40.2 us -> 39.5 us (0.983)
  starting transfers between devices: 15.3 us -> 17.6 us
  waiting for transfers between devices: 9.15 us -> 6.93 us
  other arithmetic: 0.81 us -> 0.06 us
    ppermute x1 -> x2, starting transfers between devices: 4.9 us -> 8.34 us  [shifted(): lax.ppermute(x, axis, [(i, i + by) for i in range(peers) if i + by < peers])]
    ppermute x1 -> x2, waiting for transfers between devices: 2.65 us -> 0.01 us  [shifted(): lax.ppermute(x, axis, [(i, i + by) for i in range(peers) if i + by < peers])]
    ppermute x6, starting transfers between devices: 10.3 us -> 9.23 us  [swapped(): lax.ppermute(x, axis, [(i, i ^ bit) for i in range(peers) if i ^ bit < pe...]
    mul x1 -> x0, other arithmetic: 0.73 us -> none  [per_device(): weights = residue * jnp.sqrt(-jnp.expm1(-2.0 * pole_rate))]
    ppermute x6, waiting for transfers between devices: 6.5 us -> 6.93 us  [swapped(): lax.ppermute(x, axis, [(i, i ^ bit) for i in range(peers) if i ^ bit < pe...]
    pallas_call x8 -> x10, Pallas kernels: 14 us -> 14 us  [call(): pl.pallas_call(kernel, in_specs=specs, out_specs=more.get('out_specs', ja...]
  transfers between devices with their start and end apart: 7 -> 8, of which waited for: 5 -> 4; matrix products, arithmetic and copies ran while one was open for 2% -> 0% of each run, Pallas kernels for 26% -> 28%
where the time goes in v3:
time: 39.5 us; the launch traced here: 39.3 us
  starting transfers between devices  17.6 us (45%)
  Pallas kernels  14 us (35%)
  waiting for transfers between devices  6.93 us (18%)
  between operations  0.74 us (2%)
    pallas_call x10, Pallas kernels, call(): pl.pallas_call(kernel, in_specs=specs, out_specs=more.get('out_specs', ja...  14 us
    ppermute x6, starting transfers between devices, swapped(): lax.ppermute(x, axis, [(i, i ^ bit) for i in range(peers) if i ^ bit < pe...  9.23 us
    ppermute x2, starting transfers between devices, shifted(): lax.ppermute(x, axis, [(i, i + by) for i in range(peers) if i + by < peers])  8.34 us
    ppermute x6, waiting for transfers between devices, swapped(): lax.ppermute(x, axis, [(i, i ^ bit) for i in range(peers) if i ^ bit < pe...  6.93 us
  transfers between devices with their start and end apart: 8, of which 4 were waited for; matrix products, arithmetic and copies ran while one was open for 0% of the time, Pallas kernels for 28%

profile of v3, /device:TPU:0, one launch (start us, length us, event | category | flops | bytes accessed | tf_op | source)
XLA Modules:
  0.0 39.3 jit_solution(192136174579683973)
XLA Ops:
  0.6 1.2 %shard_map.113 = (bf16[1024,128]{1,0:T(8,128)(2,1)S(1)}, bf16[128,1024]{1,0:T(8,128)(2,1)S(1)}, bf16[128,1024]{1,0:T(8,128)(2,1)S(1)}) custom-call(bf16[128,2048]{1,0:T(8,128)(2,1)} %k_hbm.2, bf16[128,2048]{1,0:T(8,128)(2,1)} %v_hbm.1), custom_call_target="tpu_custom_call" | custom-call | flops 16777216 | bytes 1048576 | tf_op jit(solution)/shard_map/pallas_call | solution.py:315
  1.9 4.9 %collective-permute-start = (bf16[1024,128]{1,0:T(8,128)(2,1)S(1)}, bf16[1024,128]{1,0:T(8,128)(2,1)S(1)}, u32[]{:S(2)}, u32[]{:S(2)}) collective-permute-start(bf16[1024,128]{1,0:T(8,128)(2,1)S(1)} %get-tuple-element.24.u_refs_0_), channel_id=1, source_target_pairs={{0,4},{4,8},{8,12},{12,16},{16,20},{20,24},{24,28},{1,5},{5,9},{9,... | collective-permute-start | bytes 786440 | tf_op jit(solution)/shard_map/ppermute | solution.py:24
  6.8 0.1 shard_map.114.u_refs_1_
  6.9 3.5 %collective-permute-start.1 = (bf16[1024,128]{1,0:T(8,128)(2,1)S(1)}, bf16[1024,128]{1,0:T(8,128)(2,1)S(1)}, u32[]{:S(2)}, u32[]{:S(2)}) collective-permute-start(bf16[1024,128]{1,0:T(8,128)(2,1)S(1)} %shard_map.114.u_refs_1_), channel_id=1, source_target_pairs={{0,4},{4,8},{8,12},{12,16},{16,20},{20,24},{24,28},{1,5},{5,9},{9,... | collective-permute-start | bytes 786440 | tf_op jit(solution)/shard_map/ppermute | solution.py:24
  10.4 7.8 %shard_map.115 = (f32[2048,128]{1,0:T(8,128)S(1)}, f32[2048,128]{1,0:T(8,128)S(1)}, f32[2048,128]{1,0:T(8,128)S(1)}, bf16[64,128,256]{2,1,0:T(8,128)(2,1)S(1)}, ...) custom-call(s32[1]{0:T(128)} %bitcast.place_ref, ...), custom_call_target="tpu_custom_call" | custom-call | flops 1073741824 | bytes 2150404 | tf_op jit(solution)/shard_map/pallas_call | solution.py:315
  18.1 0.0 collective-permute-done.halo_ref
  18.2 0.4 %shard_map.116 = (bf16[1024,128]{1,0:T(8,128)(2,1)S(1)}, f32[1024,128]{1,0:T(8,128)S(1)}, f32[1,128]{1,0:T(1,128)S(1)}) custom-call(bf16[1024,128]{1,0:T(8,128)(2,1)S(1)} %collective-permute-done.halo_ref, bf16[64,128,256]{2,1,0:T(8,128)(2,1)S(1)} %get-tuple-element.27.upper_ref, f32[2048,128]{1,0:T(8,128)S(1)} %get-tuple-element.28.base_ref, ...), custom_call_target="tpu_custom_call" | custom-call | flops 67108864 | bytes 7602176 | tf_op jit(solution)/shard_map/pallas_call | solution.py:315
  18.6 0.0 collective-permute-done.1.halo_ref
  18.6 0.4 %shard_map.117 = (bf16[1024,128]{1,0:T(8,128)(2,1)S(1)}, f32[1024,128]{1,0:T(8,128)S(1)}, f32[1,128]{1,0:T(1,128)S(1)}) custom-call(bf16[1024,128]{1,0:T(8,128)(2,1)S(1)} %collective-permute-done.1.halo_ref, bf16[64,128,256]{2,1,0:T(8,128)(2,1)S(1)} %get-tuple-element.27.upper_ref, f32[2048,128]{1,0:T(8,128)S(1)} %get-tuple-element.28.base_ref, ...), custom_call_target="tpu_custom_call" | custom-call | flops 67108864 | bytes 7602688 | tf_op jit(solution)/shard_map/pallas_call | solution.py:315
  19.0 0.5 %collective-permute-start.4 = (f32[1,128]{1,0:T(1,128)S(1)}, f32[1,128]{1,0:T(1,128)S(1)}, u32[]{:S(2)}, u32[]{:S(2)}) collective-permute-start(f32[1,128]{1,0:T(1,128)S(1)} %get-tuple-element.34.refs_0_), channel_id=1, source_target_pairs={{0,3},{1,2},{2,1},{3,0},{4,7},{5,6},{6,5},{7,4},{8,11},{9,10},{10,... | collective-permute-start | bytes 1544 | tf_op jit(solution)/shard_map/ppermute | solution.py:29
  19.5 1.2 %collective-permute-start.3 = (f32[1,128]{1,0:T(1,128)S(1)}, f32[1,128]{1,0:T(1,128)S(1)}, u32[]{:S(2)}, u32[]{:S(2)}) collective-permute-start(f32[1,128]{1,0:T(1,128)S(1)} %get-tuple-element.34.refs_0_), channel_id=1, source_target_pairs={{0,2},{1,3},{2,0},{3,1},{4,6},{5,7},{6,4},{7,5},{8,10},{9,11},{10,... | collective-permute-start | bytes 1544 | tf_op jit(solution)/shard_map/ppermute | solution.py:29
  20.7 0.3 collective-permute-start.2
  21.0 0.2 shard_map.119.refs_5_
  21.2 0.9 %collective-permute-done.4.refs_3_ = f32[1,128]{1,0:T(1,128)S(1)} collective-permute-done((f32[1,128]{1,0:T(1,128)S(1)}, f32[1,128]{1,0:T(1,128)S(1)}, u32[]{:S(2)}, u32[]{:S(2)}) %collective-permute-start.4) | collective-permute-done | bytes 544 | tf_op jit(solution)/shard_map/ppermute | solution.py:29
  22.1 1.0 %collective-permute-done.3.refs_2_ = f32[1,128]{1,0:T(1,128)S(1)} collective-permute-done((f32[1,128]{1,0:T(1,128)S(1)}, f32[1,128]{1,0:T(1,128)S(1)}, u32[]{:S(2)}, u32[]{:S(2)}) %collective-permute-start.3) | collective-permute-done | bytes 544 | tf_op jit(solution)/shard_map/ppermute | solution.py:29
  23.1 0.0 collective-permute-done.2.refs_1_
  23.1 0.3 shard_map.120
  23.4 1.6 %collective-permute-start.5 = (bf16[16,2048]{1,0:T(8,128)(2,1)S(1)}, bf16[16,2048]{1,0:T(8,128)(2,1)S(1)}, u32[]{:S(2)}, u32[]{:S(2)}) collective-permute-start(bf16[16,2048]{1,0:T(8,128)(2,1)S(1)} %get-tuple-element.38), channel_id=1, source_target_pairs={{0,4},{4,0},{8,12},{12,8},{16,20},{20,16},{24,28},{28,24},{1,5},{5... | collective-permute-start | bytes 196616 | tf_op jit(solution)/shard_map/ppermute | solution.py:29
  25.0 2.8 %collective-permute-done.5.refs_0_ = bf16[16,2048]{1,0:T(8,128)(2,1)S(1)} collective-permute-done((bf16[16,2048]{1,0:T(8,128)(2,1)S(1)}, bf16[16,2048]{1,0:T(8,128)(2,1)S(1)}, u32[]{:S(2)}, u32[]{:S(2)}) %collective-permute-start.5) | collective-permute-done | bytes 65568 | tf_op jit(solution)/shard_map/ppermute | solution.py:29
  27.7 0.0 copy-start
  27.8 2.7 %collective-permute-start.6 = (bf16[16,2048]{1,0:T(8,128)(2,1)S(1)}, bf16[16,2048]{1,0:T(8,128)(2,1)S(1)}, u32[]{:S(2)}, u32[]{:S(2)}) collective-permute-start(bf16[16,2048]{1,0:T(8,128)(2,1)S(1)} %get-tuple-element.46), channel_id=1, source_target_pairs={{0,8},{4,12},{8,0},{12,4},{16,24},{20,28},{24,16},{28,20},{1,9},{5... | collective-permute-start | bytes 196616 | tf_op jit(solution)/shard_map/ppermute | solution.py:29
  30.4 2.2 %collective-permute-done.6.refs_1_ = bf16[16,2048]{1,0:T(8,128)(2,1)S(1)} collective-permute-done((bf16[16,2048]{1,0:T(8,128)(2,1)S(1)}, bf16[16,2048]{1,0:T(8,128)(2,1)S(1)}, u32[]{:S(2)}, u32[]{:S(2)}) %collective-permute-start.6) | collective-permute-done | bytes 65568 | tf_op jit(solution)/shard_map/ppermute | solution.py:29
  32.7 3.1 %collective-permute-start.7 = (bf16[16,2048]{1,0:T(8,128)(2,1)S(1)}, bf16[16,2048]{1,0:T(8,128)(2,1)S(1)}, u32[]{:S(2)}, u32[]{:S(2)}) collective-permute-start(bf16[16,2048]{1,0:T(8,128)(2,1)S(1)} %fusion.1), channel_id=1, source_target_pairs={{0,16},{4,20},{8,24},{12,28},{16,0},{20,4},{24,8},{28,12},{1,17},{... | collective-permute-start | bytes 196616 | tf_op jit(solution)/shard_map/ppermute | solution.py:29
  35.8 0.9 %shard_map.118 = bf16[128,2048]{1,0:T(8,128)(2,1)} custom-call(bf16[1024,128]{1,0:T(8,128)(2,1)S(1)} %get-tuple-element.31.mixed_refs_0_, bf16[1024,128]{1,0:T(8,128)(2,1)S(1)} %get-tuple-element.33.mixed_refs_1_), custom_call_target="tpu_custom_call" | custom-call | flops 33554432 | bytes 524288 | tf_op jit(solution)/shard_map/pallas_call | solution.py:315
  36.7 1.4 %shard_map.121.refs_5_ = f32[128,2048]{1,0:T(8,128)S(1)} custom-call(f32[1,128]{1,0:T(1,128)S(1)} %get-tuple-element.44.scale_ref, f32[1024,128]{1,0:T(8,128)S(1)} %get-tuple-element.36.z_refs_0_, f32[1024,128]{1,0:T(8,128)S(1)} %get-tuple-element.37.z_refs_1_, bf16[64,128,256]{2,1,0:T(8,128)(2,1)S(1)} %get-tuple-element.45.square_ref), custom_call_target="tpu_custom_call" | custom-call | flops 134217728 | bytes 5243392 | tf_op jit(solution)/shard_map/pallas_call | solution.py:315
  38.1 0.0 collective-permute-done.7.refs_2_
  38.1 0.0 copy-done
  38.1 1.1 %shard_map.122 = bf16[128,2048]{1,0:T(8,128)(2,1)} custom-call(bf16[16,2048]{1,0:T(8,128)(2,1)S(1)} %collective-permute-done.5.refs_0_, bf16[16,2048]{1,0:T(8,128)(2,1)S(1)} %collective-permute-done.6.refs_1_, bf16[16,2048]{1,0:T(8,128)(2,1)S(1)} %collective-permute-done.7.refs_2_, f32[3,16,2048]{2,1,0:T(8,128)S(1)} %get-tuple-element.42.refs_3_, ...), custom_call_target="tpu_custom_call" | custom-call | flops 16777216 | bytes 3211264 | tf_op jit(solution)/shard_map/pallas_call | solution.py:315
  (2 shorter events, 0.1 us)
Async XLA Ops:
  1.9 16.3 %collective-permute-start = (bf16[1024,128]{1,0:T(8,128)(2,1)S(1)}, bf16[1024,128]{1,0:T(8,128)(2,1)S(1)}, u32[]{:S(2)}, u32[]{:S(2)}) collective-permute-start(bf16[1024,128]{1,0:T(8,128)(2,1)S(1)} %get-tuple-element.24.u_refs_0_), channel_id=1, source_target_pairs={{0,4},{4,8},{8,12},{12,16},{16,20},{20,24},{24,28},{1,5},{5,9},{9,... | collective-permute-start | bytes 786440 | tf_op jit(solution)/shard_map/ppermute | solution.py:24
  6.9 11.7 %collective-permute-start.1 = (bf16[1024,128]{1,0:T(8,128)(2,1)S(1)}, bf16[1024,128]{1,0:T(8,128)(2,1)S(1)}, u32[]{:S(2)}, u32[]{:S(2)}) collective-permute-start(bf16[1024,128]{1,0:T(8,128)(2,1)S(1)} %shard_map.114.u_refs_1_), channel_id=1, source_target_pairs={{0,4},{4,8},{8,12},{12,16},{16,20},{20,24},{24,28},{1,5},{5,9},{9,... | collective-permute-start | bytes 786440 | tf_op jit(solution)/shard_map/ppermute | solution.py:24
  19.0 3.1 %collective-permute-start.4 = (f32[1,128]{1,0:T(1,128)S(1)}, f32[1,128]{1,0:T(1,128)S(1)}, u32[]{:S(2)}, u32[]{:S(2)}) collective-permute-start(f32[1,128]{1,0:T(1,128)S(1)} %get-tuple-element.34.refs_0_), channel_id=1, source_target_pairs={{0,3},{1,2},{2,1},{3,0},{4,7},{5,6},{6,5},{7,4},{8,11},{9,10},{10,... | collective-permute-start | bytes 1544 | tf_op jit(solution)/shard_map/ppermute | solution.py:29
  19.5 3.6 %collective-permute-start.3 = (f32[1,128]{1,0:T(1,128)S(1)}, f32[1,128]{1,0:T(1,128)S(1)}, u32[]{:S(2)}, u32[]{:S(2)}) collective-permute-start(f32[1,128]{1,0:T(1,128)S(1)} %get-tuple-element.34.refs_0_), channel_id=1, source_target_pairs={{0,2},{1,3},{2,0},{3,1},{4,6},{5,7},{6,4},{7,5},{8,10},{9,11},{10,... | collective-permute-start | bytes 1544 | tf_op jit(solution)/shard_map/ppermute | solution.py:29
  20.7 2.4 %collective-permute-start.2 = (f32[1,128]{1,0:T(1,128)S(1)}, f32[1,128]{1,0:T(1,128)S(1)}, u32[]{:S(2)}, u32[]{:S(2)}) collective-permute-start(f32[1,128]{1,0:T(1,128)S(1)} %get-tuple-element.34.refs_0_), channel_id=1, source_target_pairs={{0,1},{1,0},{2,3},{3,2},{4,5},{5,4},{6,7},{7,6},{8,9},{9,8},{10,11... | collective-permute-start | bytes 1544 | tf_op jit(solution)/shard_map/ppermute | solution.py:29
  23.4 4.3 %collective-permute-start.5 = (bf16[16,2048]{1,0:T(8,128)(2,1)S(1)}, bf16[16,2048]{1,0:T(8,128)(2,1)S(1)}, u32[]{:S(2)}, u32[]{:S(2)}) collective-permute-start(bf16[16,2048]{1,0:T(8,128)(2,1)S(1)} %get-tuple-element.38), channel_id=1, source_target_pairs={{0,4},{4,0},{8,12},{12,8},{16,20},{20,16},{24,28},{28,24},{1,5},{5... | collective-permute-start | bytes 196616 | tf_op jit(solution)/shard_map/ppermute | solution.py:29
  27.7 10.4 %copy-start = (bf16[128,2048]{1,0:T(8,128)(2,1)S(1)}, bf16[128,2048]{1,0:T(8,128)(2,1)}, u32[]{:S(2)}) copy-start(bf16[128,2048]{1,0:T(8,128)(2,1)} %refs_6_.1) | copy-start | bytes 1572868
  27.8 4.9 %collective-permute-start.6 = (bf16[16,2048]{1,0:T(8,128)(2,1)S(1)}, bf16[16,2048]{1,0:T(8,128)(2,1)S(1)}, u32[]{:S(2)}, u32[]{:S(2)}) collective-permute-start(bf16[16,2048]{1,0:T(8,128)(2,1)S(1)} %get-tuple-element.46), channel_id=1, source_target_pairs={{0,8},{4,12},{8,0},{12,4},{16,24},{20,28},{24,16},{28,20},{1,9},{5... | collective-permute-start | bytes 196616 | tf_op jit(solution)/shard_map/ppermute | solution.py:29
  32.7 5.4 %collective-permute-start.7 = (bf16[16,2048]{1,0:T(8,128)(2,1)S(1)}, bf16[16,2048]{1,0:T(8,128)(2,1)S(1)}, u32[]{:S(2)}, u32[]{:S(2)}) collective-permute-start(bf16[16,2048]{1,0:T(8,128)(2,1)S(1)} %fusion.1), channel_id=1, source_target_pairs={{0,16},{4,20},{8,24},{12,28},{16,0},{20,4},{24,8},{28,12},{1,17},{... | collective-permute-start | bytes 196616 | tf_op jit(solution)/shard_map/ppermute | solution.py:29

commit v4 on v3

--- a/solution.py
+++ b/solution.py
@@ -6,6 +6,7 @@
 from jax.experimental import pallas as pl
 from jax.experimental.pallas import tpu as pltpu
 from jax.sharding import PartitionSpec as P
+
 
 LANES = 128
 GRANT = 16 << 20
@@ -14,14 +15,15 @@
 SMEM = pl.BlockSpec(memory_space=pltpu.SMEM)
 HBM = pl.BlockSpec(memory_space=pltpu.HBM)
 PARTS = 4
-CHUNKS = 2
+FIRST = 8
 SMALL, TERMS = 0.5, 10
 SPAN = 16
 
 
-def shifted(x, axis, by):
-    peers = lax.axis_size(axis)
-    return lax.ppermute(x, axis, [(i, i + by) for i in range(peers) if i + by < peers])
+def passed_on(x, close):
+    shards = lax.axis_size("ctx")
+    pairs = [(i, (i + 1) % shards) for i in range(shards if close else shards - 1)]
+    return lax.ppermute(x, "ctx", pairs)
 
 
 def swapped(x, axis, bit):
@@ -83,7 +85,7 @@
 
 
 def spans(channels):
-    size = max(LANES, channels // PARTS)
+    size = max(2 * LANES, channels // PARTS)
     return [pl.ds(start, size) for start in range(0, channels, size)]
 
 
@@ -98,7 +100,7 @@
     chunk = out_ref.shape[0]
     copies = []
     for n, to in enumerate((k_ref, v_ref) + later):
-        source = (k_hbm, v_hbm)[n % 2].at[:, pl.ds(n // 2 * chunk, chunk)]
+        source = (k_hbm, v_hbm)[n % 2].at[:, pl.ds(0, chunk) if n < 2 else pl.ds(chunk, to.shape[1])]
         copies.append(pltpu.make_async_copy(source, to, sems.at[n]))
         copies[-1].start()
     copies[0].wait()
@@ -114,8 +116,8 @@
     taps, impulse, rates, weights, lower_ref,
     gain_ref, taps_ref, rate_ref, residue_ref, resid_ref, q_ref, k_ref, sems,
 ):
-    chunk, tok = u_refs[0].shape
-    channels = chunk * len(u_refs)
+    tok = u_refs[0].shape[1]
+    channels = sum(ref.shape[0] for ref in u_refs)
     poles, groups = rate_ref.shape
     per, width = LANES // group_size, 2 * group_size
     sources = (taps_hbm, rate_hbm, residue_hbm, gain_hbm, resid_hbm, q_hbm, k_hbm)
@@ -126,7 +128,8 @@
     row = lax.broadcasted_iota(jnp.int32, (tok, tok), 0)
     col = lax.broadcasted_iota(jnp.int32, (tok, tok), 1)
     causal = jnp.where(row <= col, 1.0, 0.0).astype(BF16)
-    future = jnp.where(row <= col, 0.0, 1.0).astype(BF16)
+    live = jnp.where(place_ref[0] > 0, 1.0, 0.0)
+    future = jnp.where(row <= col, 0.0, live).astype(BF16)
 
     copies[0].wait()
     taps[...] = taps_ref[...].astype(F32)
@@ -189,8 +192,7 @@
 
     for pair in range(channels // width):
         at = pl.ds(pair * width, width)
-        u = u_refs[pair * width // chunk][pl.ds(pair * width % chunk, width), :]
-        base_ref[at, :] = pair_product(u, lower_ref[pair], group_size)
+        base_ref[at, :] = pair_product(rows_of(u_refs, pair * width, width), lower_ref[pair], group_size)
 
     for copy in copies[3:]:
         copy.wait()
@@ -200,10 +202,8 @@
         gate_ref[at, :] = gate
         base_ref[at, :] = resid_ref[:, at].T.astype(F32) + gate * base_ref[at, :]
         key_ref[at, :] = (k_ref[:, at].astype(F32) * gain_ref[i : i + 1, :].astype(F32)).T
-        entry = weights[pl.ds(i * per * poles, per * poles), :].T
-        high = entry.astype(BF16)
-        entry_ref[i, :, :LANES] = high
-        entry_ref[i, :, LANES:] = (entry - high.astype(F32)).astype(BF16)
+        enter = weights[pl.ds(i * per * poles, per * poles), :]
+        entry_ref[i // 2, :, pl.ds(i % 2 * per * poles, per * poles)] = enter.T.astype(BF16)
 
 
 def mix_kernel(group_size, first, halo_ref, upper_ref, base_ref, gate_ref, key_ref, *refs):
@@ -226,8 +226,10 @@
 
 
 def rows_of(refs, start, size):
-    chunk = refs[0].shape[0]
-    return refs[start // chunk][pl.ds(start % chunk, size), :]
+    for ref in refs:
+        if start < ref.shape[0]:
+            return ref[pl.ds(start, size), :]
+        start -= ref.shape[0]
 
 
 def turn_kernel(group_size, z_refs, zb_ref):
@@ -235,11 +237,11 @@
         zb_ref[i] = by_parity(rows_of(z_refs, i * LANES, LANES).astype(BF16).T, group_size)
 
 
-def written(tile, out_hbm, out_ref, sem):
+def written(tile, width, out_hbm, out_ref, sem):
     copies = []
     for n, part in enumerate(spans(out_ref.shape[1])):
-        for start in range(part.start, part.start + part.size, LANES):
-            out_ref[:, pl.ds(start, LANES)] = tile(start // LANES)
+        for start in range(part.start, part.start + part.size, width):
+            out_ref[:, pl.ds(start, width)] = tile(start // width)
         copies.append(pltpu.make_async_copy(out_ref.at[:, part], out_hbm.at[:, part], sem.at[n]))
         copies[-1].start()
     for copy in copies:
@@ -247,7 +249,7 @@
 
 
 def out_kernel(mixed_refs, out_hbm, out_ref, sem):
-    written(lambda i: rows_of(mixed_refs, i * LANES, LANES).T, out_hbm, out_ref, sem)
+    written(lambda i: rows_of(mixed_refs, i * LANES, LANES).T, LANES, out_hbm, out_ref, sem)
 
 
 def state_kernel(group_size, width, parts, *refs):
@@ -267,40 +269,47 @@
 
 
 def local_kernel(group_size, scale_ref, z_refs, square_ref, local_ref):
-    chunk = z_refs[0].shape[0]
     width = 2 * group_size
     scale = scale_ref[...]
-    for n, z_ref in enumerate(z_refs):
-
-        def body(i, _):
+    first = 0
+    for z_ref in z_refs:
+
+        def body(i, _, z_ref=z_ref, first=first):
             rows = []
             for pair in range(LANES // width):
                 at = pl.ds(pl.multiple_of(i * LANES + pair * width, width), width)
                 y = (z_ref[at, :] * scale).astype(BF16)
-                table = square_ref[n * (chunk // width) + i * (LANES // width) + pair]
+                table = square_ref[(first + i * LANES) // width + pair]
                 rows.append(pair_product(y, table, group_size))
-            local_ref[:, tile_of(n * (chunk // LANES) + i)] = jnp.concatenate(rows, axis=0).T
+            local_ref[:, tile_of(first // LANES + i)] = jnp.concatenate(rows, axis=0).T
             return 0
 
-        lax.fori_loop(0, chunk // LANES, body, 0, unroll=4)
+        lax.fori_loop(0, z_ref.shape[0] // LANES, body, 0, unroll=4)
+        first += z_ref.shape[0]
 
 
 def final_kernel(group_size, rounds, *refs):
     got, (factor_ref, entry_ref, local_ref, q_ref, out_hbm, out_ref, sem) = refs[:rounds], refs[rounds:]
-    poles, channels = got[0].shape
+    poles, _ = got[0].shape
     per = LANES // group_size
     group_of = lane_group((poles, LANES), group_size)
-
-    def tile(i):
+    empty = jnp.zeros((per * poles, LANES), BF16)
+
+    def spread(i):
         at = pl.ds(i * LANES, LANES)
         carried = factor_ref[0, :, at] * got[0][:, at].astype(F32)
         for step in range(1, rounds):
             carried = carried + factor_ref[step, :, at] * got[step][:, at].astype(F32)
-        spread = [jnp.where(group_of == g, carried, 0.0).astype(BF16) for g in range(per)]
-        conv = local_ref[:, at] + matmul(entry_ref[i], jnp.concatenate(spread * 2, axis=0))
+        return jnp.concatenate([jnp.where(group_of == g, carried, 0.0) for g in range(per)], axis=0).astype(BF16)
+
+    def tile(i):
+        at = pl.ds(2 * i * LANES, 2 * LANES)
+        left = jnp.concatenate([spread(2 * i), empty], axis=1)
+        right = jnp.concatenate([empty, spread(2 * i + 1)], axis=1)
+        conv = local_ref[:, at] + matmul(entry_ref[i], jnp.concatenate([left, right], axis=0))
         return (q_ref[:, at].astype(F32) * conv).astype(BF16)
 
-    written(tile, out_hbm, out_ref, sem)
+    written(tile, 2 * LANES, out_hbm, out_ref, sem)
 
 
 def held(shape, dtype):
@@ -328,7 +337,7 @@
     groups, tap_count = mr_taps.shape
     poles = pole_rate.shape[0]
     group_size = channels // groups
-    assert tap_count == tok and channels % LANES == 0 and LANES % (2 * group_size) == 0
+    assert tap_count == tok and channels % (16 * LANES) == 0 and LANES % (2 * group_size) == 0
     tiles, per = channels // LANES, LANES // group_size
     shards = lax.axis_size("ctx")
     bits = [1 << b for b in range((shards - 1).bit_length())]
@@ -336,21 +345,18 @@
     place = lax.axis_index("ctx").astype(jnp.int32).reshape(1)
     work = 4 * tok * tok * channels
 
-    chunk = channels // CHUNKS
-    firsts = range(0, channels, chunk)
-    part = pltpu.VMEM((tok, chunk), BF16)
+    sizes = [channels * FIRST // 16, channels - channels * FIRST // 16]
+    firsts = [0, sizes[0]]
     rows = pltpu.VMEM((tok, channels), BF16)
+    part = pltpu.VMEM((tok, sizes[0]), BF16)
     sem = pltpu.SemaphoreType.DMA((PARTS,))
-    late = [held((tok, chunk), BF16)] * (2 * CHUNKS - 2)
-    outs = call(
-        first_kernel, [held((chunk, tok), BF16)] + late, [part, part, pltpu.SemaphoreType.DMA((2 * CHUNKS,))],
-        work // 8, k_mr, v_mr, in_specs=[HBM, HBM],
-    )
-    u = [outs[0]]
-    halo = [shifted(u[0], "ctx", 1)]
-    for n in range(1, len(outs), 2):
-        u.append(call(gated, held((chunk, tok), BF16), [], work // 8, *outs[n : n + 2]))
-        halo.append(shifted(u[-1], "ctx", 1))
+    u0, k1, v1 = call(
+        first_kernel, [held((sizes[0], tok), BF16)] + [held((tok, sizes[1]), BF16)] * 2,
+        [part, part, pltpu.SemaphoreType.DMA((4,))], work // 8, k_mr, v_mr, in_specs=[HBM, HBM],
+    )
+    halo = [passed_on(u0, True)]
+    u = [u0, call(gated, held((sizes[1], tok), BF16), [], work // 8, k1, v1)]
+    halo.append(passed_on(u[1], False))
 
     tall = held((channels, tok), F32)
     table = held((groups // 2, tok, 2 * tok), BF16)
@@ -360,7 +366,7 @@
         (
             tall, tall, tall, table, table,
             held((tiles, per // 2 * poles, 2 * tok), F32),
-            held((tiles, tok, 2 * per * poles), BF16),
+            held((tiles // 2, tok, 2 * per * poles), BF16),
             steps, steps, steps,
         ),
         [
@@ -377,9 +383,9 @@
     for first, past in zip(firsts, halo):
         outs = call(
             functools.partial(mix_kernel, group_size, first),
-            (held((chunk, tok), BF16), held((chunk, tok), F32), held((1, tok), F32)),
+            (held(past.shape, BF16), held(past.shape, F32), held((1, tok), F32)),
             [],
-            work // CHUNKS,
+            work // 2,
             past, upper, base, gate, key, *square_sum,
         )
         mixed_t.append(outs[0])
@@ -425,6 +431,4 @@
 def solution(mesh):
     whole, tables = P("ctx", "tp"), P(None, "tp")
     placed = (whole,) * 4 + (P("tp", None), P("tp")) + (whole,) * 2 + (tables,) * 2
-    return jax.shard_map(
-        per_device, mesh=mesh, in_specs=placed, out_specs=(whole, whole), check_vma=False
-    )
+    return jax.shard_map(per_device, mesh=mesh, in_specs=placed, out_specs=(whole, whole), check_vma=False)

time: 39.5 us -> 37.5 us (0.949)
  starting transfers between devices: 17.6 us -> 16.1 us
    ppermute x2, starting transfers between devices: 8.34 us -> 6.49 us  [passed_on(): return lax.ppermute(x, 'ctx', pairs)]
where the time goes in v4:
time: 37.5 us; the launch traced here: 37.4 us
  starting transfers between devices  16.1 us (43%)
  Pallas kernels  13.7 us (37%)
  waiting for transfers between devices  6.8 us (18%)
  between operations  0.73 us (2%)
    pallas_call x10, Pallas kernels, call(): pl.pallas_call(kernel, in_specs=specs, out_specs=more.get('out_specs', ja...  13.7 us
    ppermute x6, starting transfers between devices, swapped(): lax.ppermute(x, axis, [(i, i ^ bit) for i in range(peers) if i ^ bit < pe...  9.62 us
    ppermute x6, waiting for transfers between devices, swapped(): lax.ppermute(x, axis, [(i, i ^ bit) for i in range(peers) if i ^ bit < pe...  6.79 us
    ppermute x2, starting transfers between devices, passed_on(): return lax.ppermute(x, 'ctx', pairs)  6.49 us
  transfers between devices with their start and end apart: 8, of which 4 were waited for; matrix products, arithmetic and copies ran while one was open for 0% of the time, Pallas kernels for 28%

profile of v4, /device:TPU:0, one launch (start us, length us, event | category | flops | bytes accessed | tf_op | source)
XLA Modules:
  0.0 37.4 jit_solution(2140541078854131246)
XLA Ops:
  0.6 1.2 %shard_map.113 = (bf16[1024,128]{1,0:T(8,128)(2,1)S(1)}, bf16[128,1024]{1,0:T(8,128)(2,1)S(1)}, bf16[128,1024]{1,0:T(8,128)(2,1)S(1)}) custom-call(bf16[128,2048]{1,0:T(8,128)(2,1)} %k_hbm.2, bf16[128,2048]{1,0:T(8,128)(2,1)} %v_hbm.1), custom_call_target="tpu_custom_call" | custom-call | flops 16777216 | bytes 1048576 | tf_op jit(solution)/shard_map/pallas_call | solution.py:324
  1.9 3.0 %collective-permute-start = (bf16[1024,128]{1,0:T(8,128)(2,1)S(1)}, bf16[1024,128]{1,0:T(8,128)(2,1)S(1)}, u32[]{:S(2)}, u32[]{:S(2)}) collective-permute-start(bf16[1024,128]{1,0:T(8,128)(2,1)S(1)} %get-tuple-element.24.u_refs_0_), channel_id=1, source_target_pairs={{0,4},{4,8},{8,12},{12,16},{16,20},{20,24},{24,28},{28,0},{1,5},{5... | collective-permute-start | bytes 786440 | tf_op jit(solution)/shard_map/ppermute | solution.py:26
  4.9 0.1 shard_map.114.u_refs_1_
  5.0 3.5 %collective-permute-start.1 = (bf16[1024,128]{1,0:T(8,128)(2,1)S(1)}, bf16[1024,128]{1,0:T(8,128)(2,1)S(1)}, u32[]{:S(2)}, u32[]{:S(2)}) collective-permute-start(bf16[1024,128]{1,0:T(8,128)(2,1)S(1)} %shard_map.114.u_refs_1_), channel_id=1, source_target_pairs={{0,4},{4,8},{8,12},{12,16},{16,20},{20,24},{24,28},{1,5},{5,9},{9,... | collective-permute-start | bytes 786440 | tf_op jit(solution)/shard_map/ppermute | solution.py:26
  8.5 7.6 %shard_map.115 = (f32[2048,128]{1,0:T(8,128)S(1)}, f32[2048,128]{1,0:T(8,128)S(1)}, f32[2048,128]{1,0:T(8,128)S(1)}, bf16[64,128,256]{2,1,0:T(8,128)(2,1)S(1)}, ...) custom-call(s32[1]{0:T(128)} %bitcast.place_ref, ...), custom_call_target="tpu_custom_call" | custom-call | flops 1073741824 | bytes 2150404 | tf_op jit(solution)/shard_map/pallas_call | solution.py:324
  16.1 0.0 collective-permute-done.halo_ref
  16.1 0.4 %shard_map.116 = (bf16[1024,128]{1,0:T(8,128)(2,1)S(1)}, f32[1024,128]{1,0:T(8,128)S(1)}, f32[1,128]{1,0:T(1,128)S(1)}) custom-call(bf16[1024,128]{1,0:T(8,128)(2,1)S(1)} %collective-permute-done.halo_ref, bf16[64,128,256]{2,1,0:T(8,128)(2,1)S(1)} %get-tuple-element.27.upper_ref, f32[2048,128]{1,0:T(8,128)S(1)} %get-tuple-element.28.base_ref, ...), custom_call_target="tpu_custom_call" | custom-call | flops 67108864 | bytes 7602176 | tf_op jit(solution)/shard_map/pallas_call | solution.py:324
  16.5 0.0 collective-permute-done.1.halo_ref
  16.5 0.4 %shard_map.117 = (bf16[1024,128]{1,0:T(8,128)(2,1)S(1)}, f32[1024,128]{1,0:T(8,128)S(1)}, f32[1,128]{1,0:T(1,128)S(1)}) custom-call(bf16[1024,128]{1,0:T(8,128)(2,1)S(1)} %collective-permute-done.1.halo_ref, bf16[64,128,256]{2,1,0:T(8,128)(2,1)S(1)} %get-tuple-element.27.upper_ref, f32[2048,128]{1,0:T(8,128)S(1)} %get-tuple-element.28.base_ref, ...), custom_call_target="tpu_custom_call" | custom-call | flops 67108864 | bytes 7602688 | tf_op jit(solution)/shard_map/pallas_call | solution.py:324
  16.9 0.5 %collective-permute-start.4 = (f32[1,128]{1,0:T(1,128)S(1)}, f32[1,128]{1,0:T(1,128)S(1)}, u32[]{:S(2)}, u32[]{:S(2)}) collective-permute-start(f32[1,128]{1,0:T(1,128)S(1)} %get-tuple-element.34.refs_0_), channel_id=1, source_target_pairs={{0,3},{1,2},{2,1},{3,0},{4,7},{5,6},{6,5},{7,4},{8,11},{9,10},{10,... | collective-permute-start | bytes 1544 | tf_op jit(solution)/shard_map/ppermute | solution.py:31
  17.4 1.2 %collective-permute-start.3 = (f32[1,128]{1,0:T(1,128)S(1)}, f32[1,128]{1,0:T(1,128)S(1)}, u32[]{:S(2)}, u32[]{:S(2)}) collective-permute-start(f32[1,128]{1,0:T(1,128)S(1)} %get-tuple-element.34.refs_0_), channel_id=1, source_target_pairs={{0,2},{1,3},{2,0},{3,1},{4,6},{5,7},{6,4},{7,5},{8,10},{9,11},{10,... | collective-permute-start | bytes 1544 | tf_op jit(solution)/shard_map/ppermute | solution.py:31
  18.6 0.3 collective-permute-start.2
  18.9 0.2 shard_map.119.refs_5_
  19.1 0.9 %collective-permute-done.4.refs_3_ = f32[1,128]{1,0:T(1,128)S(1)} collective-permute-done((f32[1,128]{1,0:T(1,128)S(1)}, f32[1,128]{1,0:T(1,128)S(1)}, u32[]{:S(2)}, u32[]{:S(2)}) %collective-permute-start.4) | collective-permute-done | bytes 544 | tf_op jit(solution)/shard_map/ppermute | solution.py:31
  20.0 1.0 %collective-permute-done.3.refs_2_ = f32[1,128]{1,0:T(1,128)S(1)} collective-permute-done((f32[1,128]{1,0:T(1,128)S(1)}, f32[1,128]{1,0:T(1,128)S(1)}, u32[]{:S(2)}, u32[]{:S(2)}) %collective-permute-start.3) | collective-permute-done | bytes 544 | tf_op jit(solution)/shard_map/ppermute | solution.py:31
  21.0 0.0 collective-permute-done.2.refs_1_
  21.0 0.3 shard_map.120
  21.3 1.8 %collective-permute-start.5 = (bf16[16,2048]{1,0:T(8,128)(2,1)S(1)}, bf16[16,2048]{1,0:T(8,128)(2,1)S(1)}, u32[]{:S(2)}, u32[]{:S(2)}) collective-permute-start(bf16[16,2048]{1,0:T(8,128)(2,1)S(1)} %get-tuple-element.38), channel_id=1, source_target_pairs={{0,4},{4,0},{8,12},{12,8},{16,20},{20,16},{24,28},{28,24},{1,5},{5... | collective-permute-start | bytes 196616 | tf_op jit(solution)/shard_map/ppermute | solution.py:31
  23.1 2.6 %collective-permute-done.5.refs_0_ = bf16[16,2048]{1,0:T(8,128)(2,1)S(1)} collective-permute-done((bf16[16,2048]{1,0:T(8,128)(2,1)S(1)}, bf16[16,2048]{1,0:T(8,128)(2,1)S(1)}, u32[]{:S(2)}, u32[]{:S(2)}) %collective-permute-start.5) | collective-permute-done | bytes 65568 | tf_op jit(solution)/shard_map/ppermute | solution.py:31
  25.8 0.0 copy-start
  25.8 2.8 %collective-permute-start.6 = (bf16[16,2048]{1,0:T(8,128)(2,1)S(1)}, bf16[16,2048]{1,0:T(8,128)(2,1)S(1)}, u32[]{:S(2)}, u32[]{:S(2)}) collective-permute-start(bf16[16,2048]{1,0:T(8,128)(2,1)S(1)} %get-tuple-element.46), channel_id=1, source_target_pairs={{0,8},{4,12},{8,0},{12,4},{16,24},{20,28},{24,16},{28,20},{1,9},{5... | collective-permute-start | bytes 196616 | tf_op jit(solution)/shard_map/ppermute | solution.py:31
  28.6 2.2 %collective-permute-done.6.refs_1_ = bf16[16,2048]{1,0:T(8,128)(2,1)S(1)} collective-permute-done((bf16[16,2048]{1,0:T(8,128)(2,1)S(1)}, bf16[16,2048]{1,0:T(8,128)(2,1)S(1)}, u32[]{:S(2)}, u32[]{:S(2)}) %collective-permute-start.6) | collective-permute-done | bytes 65568 | tf_op jit(solution)/shard_map/ppermute | solution.py:31
  30.9 3.1 %collective-permute-start.7 = (bf16[16,2048]{1,0:T(8,128)(2,1)S(1)}, bf16[16,2048]{1,0:T(8,128)(2,1)S(1)}, u32[]{:S(2)}, u32[]{:S(2)}) collective-permute-start(bf16[16,2048]{1,0:T(8,128)(2,1)S(1)} %fusion.1), channel_id=1, source_target_pairs={{0,16},{4,20},{8,24},{12,28},{16,0},{20,4},{24,8},{28,12},{1,17},{... | collective-permute-start | bytes 196616 | tf_op jit(solution)/shard_map/ppermute | solution.py:31
  34.0 0.9 %shard_map.118 = bf16[128,2048]{1,0:T(8,128)(2,1)} custom-call(bf16[1024,128]{1,0:T(8,128)(2,1)S(1)} %get-tuple-element.31.mixed_refs_0_, bf16[1024,128]{1,0:T(8,128)(2,1)S(1)} %get-tuple-element.33.mixed_refs_1_), custom_call_target="tpu_custom_call" | custom-call | flops 33554432 | bytes 524288 | tf_op jit(solution)/shard_map/pallas_call | solution.py:324
  34.9 1.4 %shard_map.121.refs_5_ = f32[128,2048]{1,0:T(8,128)S(1)} custom-call(f32[1,128]{1,0:T(1,128)S(1)} %get-tuple-element.44.scale_ref, f32[1024,128]{1,0:T(8,128)S(1)} %get-tuple-element.36.z_refs_0_, f32[1024,128]{1,0:T(8,128)S(1)} %get-tuple-element.37.z_refs_1_, bf16[64,128,256]{2,1,0:T(8,128)(2,1)S(1)} %get-tuple-element.45.square_ref), custom_call_target="tpu_custom_call" | custom-call | flops 134217728 | bytes 5243392 | tf_op jit(solution)/shard_map/pallas_call | solution.py:324
  36.3 0.0 collective-permute-done.7.refs_2_
  36.3 0.0 copy-done
  36.3 1.1 %shard_map.122 = bf16[128,2048]{1,0:T(8,128)(2,1)} custom-call(bf16[16,2048]{1,0:T(8,128)(2,1)S(1)} %collective-permute-done.5.refs_0_, bf16[16,2048]{1,0:T(8,128)(2,1)S(1)} %collective-permute-done.6.refs_1_, bf16[16,2048]{1,0:T(8,128)(2,1)S(1)} %collective-permute-done.7.refs_2_, f32[3,16,2048]{2,1,0:T(8,128)S(1)} %get-tuple-element.42.refs_3_, ...), custom_call_target="tpu_custom_call" | custom-call | flops 16777216 | bytes 2686976 | tf_op jit(solution)/shard_map/pallas_call | solution.py:324
  (2 shorter events, 0.1 us)
Async XLA Ops:
  1.9 14.2 %collective-permute-start = (bf16[1024,128]{1,0:T(8,128)(2,1)S(1)}, bf16[1024,128]{1,0:T(8,128)(2,1)S(1)}, u32[]{:S(2)}, u32[]{:S(2)}) collective-permute-start(bf16[1024,128]{1,0:T(8,128)(2,1)S(1)} %get-tuple-element.24.u_refs_0_), channel_id=1, source_target_pairs={{0,4},{4,8},{8,12},{12,16},{16,20},{20,24},{24,28},{28,0},{1,5},{5... | collective-permute-start | bytes 786440 | tf_op jit(solution)/shard_map/ppermute | solution.py:26
  5.0 11.5 %collective-permute-start.1 = (bf16[1024,128]{1,0:T(8,128)(2,1)S(1)}, bf16[1024,128]{1,0:T(8,128)(2,1)S(1)}, u32[]{:S(2)}, u32[]{:S(2)}) collective-permute-start(bf16[1024,128]{1,0:T(8,128)(2,1)S(1)} %shard_map.114.u_refs_1_), channel_id=1, source_target_pairs={{0,4},{4,8},{8,12},{12,16},{16,20},{20,24},{24,28},{1,5},{5,9},{9,... | collective-permute-start | bytes 786440 | tf_op jit(solution)/shard_map/ppermute | solution.py:26
  16.9 3.1 %collective-permute-start.4 = (f32[1,128]{1,0:T(1,128)S(1)}, f32[1,128]{1,0:T(1,128)S(1)}, u32[]{:S(2)}, u32[]{:S(2)}) collective-permute-start(f32[1,128]{1,0:T(1,128)S(1)} %get-tuple-element.34.refs_0_), channel_id=1, source_target_pairs={{0,3},{1,2},{2,1},{3,0},{4,7},{5,6},{6,5},{7,4},{8,11},{9,10},{10,... | collective-permute-start | bytes 1544 | tf_op jit(solution)/shard_map/ppermute | solution.py:31
  17.4 3.6 %collective-permute-start.3 = (f32[1,128]{1,0:T(1,128)S(1)}, f32[1,128]{1,0:T(1,128)S(1)}, u32[]{:S(2)}, u32[]{:S(2)}) collective-permute-start(f32[1,128]{1,0:T(1,128)S(1)} %get-tuple-element.34.refs_0_), channel_id=1, source_target_pairs={{0,2},{1,3},{2,0},{3,1},{4,6},{5,7},{6,4},{7,5},{8,10},{9,11},{10,... | collective-permute-start | bytes 1544 | tf_op jit(solution)/shard_map/ppermute | solution.py:31
  18.6 2.4 %collective-permute-start.2 = (f32[1,128]{1,0:T(1,128)S(1)}, f32[1,128]{1,0:T(1,128)S(1)}, u32[]{:S(2)}, u32[]{:S(2)}) collective-permute-start(f32[1,128]{1,0:T(1,128)S(1)} %get-tuple-element.34.refs_0_), channel_id=1, source_target_pairs={{0,1},{1,0},{2,3},{3,2},{4,5},{5,4},{6,7},{7,6},{8,9},{9,8},{10,11... | collective-permute-start | bytes 1544 | tf_op jit(solution)/shard_map/ppermute | solution.py:31
  21.3 4.4 %collective-permute-start.5 = (bf16[16,2048]{1,0:T(8,128)(2,1)S(1)}, bf16[16,2048]{1,0:T(8,128)(2,1)S(1)}, u32[]{:S(2)}, u32[]{:S(2)}) collective-permute-start(bf16[16,2048]{1,0:T(8,128)(2,1)S(1)} %get-tuple-element.38), channel_id=1, source_target_pairs={{0,4},{4,0},{8,12},{12,8},{16,20},{20,16},{24,28},{28,24},{1,5},{5... | collective-permute-start | bytes 196616 | tf_op jit(solution)/shard_map/ppermute | solution.py:31
  25.8 10.5 %copy-start = (bf16[128,2048]{1,0:T(8,128)(2,1)S(1)}, bf16[128,2048]{1,0:T(8,128)(2,1)}, u32[]{:S(2)}) copy-start(bf16[128,2048]{1,0:T(8,128)(2,1)} %refs_6_.1) | copy-start | bytes 1572868
  25.8 5.0 %collective-permute-start.6 = (bf16[16,2048]{1,0:T(8,128)(2,1)S(1)}, bf16[16,2048]{1,0:T(8,128)(2,1)S(1)}, u32[]{:S(2)}, u32[]{:S(2)}) collective-permute-start(bf16[16,2048]{1,0:T(8,128)(2,1)S(1)} %get-tuple-element.46), channel_id=1, source_target_pairs={{0,8},{4,12},{8,0},{12,4},{16,24},{20,28},{24,16},{28,20},{1,9},{5... | collective-permute-start | bytes 196616 | tf_op jit(solution)/shard_map/ppermute | solution.py:31
  30.9 5.4 %collective-permute-start.7 = (bf16[16,2048]{1,0:T(8,128)(2,1)S(1)}, bf16[16,2048]{1,0:T(8,128)(2,1)S(1)}, u32[]{:S(2)}, u32[]{:S(2)}) collective-permute-start(bf16[16,2048]{1,0:T(8,128)(2,1)S(1)} %fusion.1), channel_id=1, source_target_pairs={{0,16},{4,20},{8,24},{12,28},{16,0},{20,4},{24,8},{28,12},{1,17},{... | collective-permute-start | bytes 196616 | tf_op jit(solution)/shard_map/ppermute | solution.py:31

commit v5 on v4

--- a/solution.py
+++ b/solution.py
@@ -62,10 +62,13 @@
     return jnp.dot(a, b, preferred_element_type=F32)
 
 
-def pair_product(x, table, group_size):
-    out = matmul(x, table)
+def own_half(out, group_size):
     tok = out.shape[1] // 2
     return jnp.concatenate([out[:group_size, :tok], out[group_size:, tok:]], axis=0)
+
+
+def pair_product(x, table, group_size):
+    return own_half(matmul(x, table), group_size)
 
 
 def turned(row, size):
@@ -112,8 +115,8 @@
 
 def prep_kernel(
     group_size, bits, place_ref, u_refs, gain_hbm, taps_hbm, rate_hbm, residue_hbm, resid_hbm, q_hbm, k_hbm,
-    base_ref, gate_ref, key_ref, upper_ref, square_ref, leave_ref, entry_ref, factor_ref, keep_ref, take_ref,
-    taps, impulse, rates, weights, lower_ref,
+    base_ref, gate_ref, key_ref, upper_ref, impulse, leave_ref, entry_ref, factor_ref, keep_ref, take_ref,
+    taps, rates, weights, lower_ref,
     gain_ref, taps_ref, rate_ref, residue_ref, resid_ref, q_ref, k_ref, sems,
 ):
     tok = u_refs[0].shape[1]
@@ -182,14 +185,6 @@
 
     lax.fori_loop(0, channels // LANES, decays, 0, unroll=2)
 
-    def square_tables(i, _):
-        for k in range(SPAN):
-            ring = turned(impulse[pl.ds(i * SPAN + k, 1), :], tok)
-            square_ref[i * (SPAN // 2) + k // 2, :, pl.ds(k % 2 * tok, tok)] = ring * causal
-        return 0
-
-    lax.fori_loop(0, groups // SPAN, square_tables, 0)
-
     for pair in range(channels // width):
         at = pl.ds(pair * width, width)
         base_ref[at, :] = pair_product(rows_of(u_refs, pair * width, width), lower_ref[pair], group_size)
@@ -204,6 +199,21 @@
         key_ref[at, :] = (k_ref[:, at].astype(F32) * gain_ref[i : i + 1, :].astype(F32)).T
         enter = weights[pl.ds(i * per * poles, per * poles), :]
         entry_ref[i // 2, :, pl.ds(i % 2 * per * poles, per * poles)] = enter.T.astype(BF16)
+
+
+def square_kernel(impulse_ref, square_ref):
+    groups, tok = impulse_ref.shape
+    row = lax.broadcasted_iota(jnp.int32, (tok, tok), 0)
+    col = lax.broadcasted_iota(jnp.int32, (tok, tok), 1)
+    causal = jnp.where(row <= col, 1.0, 0.0).astype(BF16)
+
+    def body(i, _):
+        for k in range(SPAN):
+            ring = turned(impulse_ref[pl.ds(i * SPAN + k, 1), :], tok)
+            square_ref[i * (SPAN // 2) + k // 2, :, pl.ds(k % 2 * tok, tok)] = ring * causal
+        return 0
+
+    lax.fori_loop(0, groups // SPAN, body, 0)
 
 
 def mix_kernel(group_size, first, halo_ref, upper_ref, base_ref, gate_ref, key_ref, *refs):
@@ -278,9 +288,12 @@
             rows = []
             for pair in range(LANES // width):
                 at = pl.ds(pl.multiple_of(i * LANES + pair * width, width), width)
-                y = (z_ref[at, :] * scale).astype(BF16)
+                y = z_ref[at, :] * scale
+                high = y.astype(BF16)
+                low = (y - high.astype(F32)).astype(BF16)
                 table = square_ref[(first + i * LANES) // width + pair]
-                rows.append(pair_product(y, table, group_size))
+                out = matmul(jnp.concatenate([high, low], axis=0), table)
+                rows.append(own_half(out[:width] + out[width:], group_size))
             local_ref[:, tile_of(first // LANES + i)] = jnp.concatenate(rows, axis=0).T
             return 0
 
@@ -361,16 +374,16 @@
     tall = held((channels, tok), F32)
     table = held((groups // 2, tok, 2 * tok), BF16)
     steps = held((rounds, poles, channels), F32)
-    base, gate, key, upper, square, leave, entry, factor, keep, take = call(
+    base, gate, key, upper, impulse, leave, entry, factor, keep, take = call(
         functools.partial(prep_kernel, group_size, bits),
         (
-            tall, tall, tall, table, table,
+            tall, tall, tall, table, held((groups, tok), F32),
             held((tiles, per // 2 * poles, 2 * tok), F32),
             held((tiles // 2, tok, 2 * per * poles), BF16),
             steps, steps, steps,
         ),
         [
-            pltpu.VMEM((groups, tok), F32), pltpu.VMEM((groups, tok), F32), pltpu.VMEM((groups * poles, tok), F32),
+            pltpu.VMEM((groups, tok), F32), pltpu.VMEM((groups * poles, tok), F32),
             pltpu.VMEM((groups * poles, tok), F32), pltpu.VMEM(table.shape, BF16), pltpu.VMEM((tiles, LANES), BF16),
             pltpu.VMEM((groups, tok), BF16), pltpu.VMEM((poles, groups), F32), pltpu.VMEM((poles, groups), F32),
             rows, rows, rows, pltpu.SemaphoreType.DMA((7,)),
@@ -404,6 +417,7 @@
         work // 8,
         *sums, leave, zb,
     )
+    square = call(square_kernel, table, [], work, impulse)
     local = call(
         functools.partial(local_kernel, group_size),
         held((tok, channels), F32),

time: 37.5 us -> 39.3 us (1.048)
  waiting for transfers between devices: 6.8 us -> 7.74 us
  starting transfers between devices: 16.1 us -> 16.8 us
    ppermute x2, waiting for transfers between devices: 0.01 us -> 1.25 us  [passed_on(): return lax.ppermute(x, 'ctx', pairs)]
    ppermute x6, starting transfers between devices: 9.62 us -> 10.4 us  [swapped(): lax.ppermute(x, axis, [(i, i ^ bit) for i in range(peers) if i ^ bit < pe...]
    pallas_call x10 -> x11, Pallas kernels: 13.7 us -> 13.7 us  [call(): pl.pallas_call(kernel, in_specs=specs, out_specs=more.get('out_specs', ja...]
  transfers between devices with their start and end apart: 8 -> 8, of which waited for: 4 -> 5; matrix products, arithmetic and copies ran while one was open for 0% -> 0% of each run, Pallas kernels for 28% -> 27%
where the time goes in v5:
time: 39.3 us; the launch traced here: 39.1 us
  starting transfers between devices  16.8 us (43%)
  Pallas kernels  13.7 us (35%)
  waiting for transfers between devices  7.74 us (20%)
  between operations  0.74 us (2%)
    pallas_call x11, Pallas kernels, call(): pl.pallas_call(kernel, in_specs=specs, out_specs=more.get('out_specs', ja...  13.7 us
    ppermute x6, starting transfers between devices, swapped(): lax.ppermute(x, axis, [(i, i ^ bit) for i in range(peers) if i ^ bit < pe...  10.4 us
    ppermute x6, waiting for transfers between devices, swapped(): lax.ppermute(x, axis, [(i, i ^ bit) for i in range(peers) if i ^ bit < pe...  6.5 us
    ppermute x2, starting transfers between devices, passed_on(): return lax.ppermute(x, 'ctx', pairs)  6.49 us
    ppermute x2, waiting for transfers between devices, passed_on(): return lax.ppermute(x, 'ctx', pairs)  1.25 us
  transfers between devices with their start and end apart: 8, of which 5 were waited for; matrix products, arithmetic and copies ran while one was open for 0% of the time, Pallas kernels for 27%

profile of v5, /device:TPU:0, one launch (start us, length us, event | category | flops | bytes accessed | tf_op | source)
XLA Modules:
  0.0 39.1 jit_solution(9336797515215946588)
XLA Ops:
  0.6 1.2 %shard_map.113 = (bf16[1024,128]{1,0:T(8,128)(2,1)S(1)}, bf16[128,1024]{1,0:T(8,128)(2,1)S(1)}, bf16[128,1024]{1,0:T(8,128)(2,1)S(1)}) custom-call(bf16[128,2048]{1,0:T(8,128)(2,1)} %k_hbm.2, bf16[128,2048]{1,0:T(8,128)(2,1)} %v_hbm.1), custom_call_target="tpu_custom_call" | custom-call | flops 16777216 | bytes 1048576 | tf_op jit(solution)/shard_map/pallas_call | solution.py:337
  1.9 3.0 %collective-permute-start = (bf16[1024,128]{1,0:T(8,128)(2,1)S(1)}, bf16[1024,128]{1,0:T(8,128)(2,1)S(1)}, u32[]{:S(2)}, u32[]{:S(2)}) collective-permute-start(bf16[1024,128]{1,0:T(8,128)(2,1)S(1)} %get-tuple-element.24.u_refs_0_), channel_id=1, source_target_pairs={{0,4},{4,8},{8,12},{12,16},{16,20},{20,24},{24,28},{28,0},{1,5},{5... | collective-permute-start | bytes 786440 | tf_op jit(solution)/shard_map/ppermute | solution.py:26
  4.9 0.1 shard_map.114.u_refs_1_
  5.0 3.5 %collective-permute-start.1 = (bf16[1024,128]{1,0:T(8,128)(2,1)S(1)}, bf16[1024,128]{1,0:T(8,128)(2,1)S(1)}, u32[]{:S(2)}, u32[]{:S(2)}) collective-permute-start(bf16[1024,128]{1,0:T(8,128)(2,1)S(1)} %shard_map.114.u_refs_1_), channel_id=1, source_target_pairs={{0,4},{4,8},{8,12},{12,16},{16,20},{20,24},{24,28},{1,5},{5,9},{9,... | collective-permute-start | bytes 786440 | tf_op jit(solution)/shard_map/ppermute | solution.py:26
  8.5 5.9 %shard_map.115 = (f32[2048,128]{1,0:T(8,128)S(1)}, f32[2048,128]{1,0:T(8,128)S(1)}, f32[2048,128]{1,0:T(8,128)S(1)}, bf16[64,128,256]{2,1,0:T(8,128)(2,1)S(1)}, ...) custom-call(s32[1]{0:T(128)} %bitcast.place_ref, ...), custom_call_target="tpu_custom_call" | custom-call | flops 1073741824 | bytes 2150404 | tf_op jit(solution)/shard_map/pallas_call | solution.py:337
  14.4 0.0 collective-permute-done.halo_ref
  14.4 0.4 %shard_map.116 = (bf16[1024,128]{1,0:T(8,128)(2,1)S(1)}, f32[1024,128]{1,0:T(8,128)S(1)}, f32[1,128]{1,0:T(1,128)S(1)}) custom-call(bf16[1024,128]{1,0:T(8,128)(2,1)S(1)} %collective-permute-done.halo_ref, bf16[64,128,256]{2,1,0:T(8,128)(2,1)S(1)} %get-tuple-element.27.upper_ref, f32[2048,128]{1,0:T(8,128)S(1)} %get-tuple-element.28.base_ref, ...), custom_call_target="tpu_custom_call" | custom-call | flops 67108864 | bytes 7602176 | tf_op jit(solution)/shard_map/pallas_call | solution.py:337
  14.8 1.2 %collective-permute-done.1.halo_ref = bf16[1024,128]{1,0:T(8,128)(2,1)S(1)} collective-permute-done((bf16[1024,128]{1,0:T(8,128)(2,1)S(1)}, bf16[1024,128]{1,0:T(8,128)(2,1)S(1)}, u32[]{:S(2)}, u32[]{:S(2)}) %collective-permute-start.1) | collective-permute-done | bytes 262176 | tf_op jit(solution)/shard_map/ppermute | solution.py:26
  16.1 0.4 %shard_map.117 = (bf16[1024,128]{1,0:T(8,128)(2,1)S(1)}, f32[1024,128]{1,0:T(8,128)S(1)}, f32[1,128]{1,0:T(1,128)S(1)}) custom-call(bf16[1024,128]{1,0:T(8,128)(2,1)S(1)} %collective-permute-done.1.halo_ref, bf16[64,128,256]{2,1,0:T(8,128)(2,1)S(1)} %get-tuple-element.27.upper_ref, f32[2048,128]{1,0:T(8,128)S(1)} %get-tuple-element.28.base_ref, ...), custom_call_target="tpu_custom_call" | custom-call | flops 67108864 | bytes 7602688 | tf_op jit(solution)/shard_map/pallas_call | solution.py:337
  16.5 0.2 collective-permute-start.4
  16.7 1.5 %collective-permute-start.3 = (f32[1,128]{1,0:T(1,128)S(1)}, f32[1,128]{1,0:T(1,128)S(1)}, u32[]{:S(2)}, u32[]{:S(2)}) collective-permute-start(f32[1,128]{1,0:T(1,128)S(1)} %get-tuple-element.34.refs_0_), channel_id=1, source_target_pairs={{0,2},{1,3},{2,0},{3,1},{4,6},{5,7},{6,4},{7,5},{8,10},{9,11},{10,... | collective-permute-start | bytes 1544 | tf_op jit(solution)/shard_map/ppermute | solution.py:31
  18.2 0.3 collective-permute-start.2
  18.4 0.2 shard_map.119.refs_5_
  18.6 0.9 %collective-permute-done.4.refs_3_ = f32[1,128]{1,0:T(1,128)S(1)} collective-permute-done((f32[1,128]{1,0:T(1,128)S(1)}, f32[1,128]{1,0:T(1,128)S(1)}, u32[]{:S(2)}, u32[]{:S(2)}) %collective-permute-start.4) | collective-permute-done | bytes 544 | tf_op jit(solution)/shard_map/ppermute | solution.py:31
  19.6 0.7 %collective-permute-done.3.refs_2_ = f32[1,128]{1,0:T(1,128)S(1)} collective-permute-done((f32[1,128]{1,0:T(1,128)S(1)}, f32[1,128]{1,0:T(1,128)S(1)}, u32[]{:S(2)}, u32[]{:S(2)}) %collective-permute-start.3) | collective-permute-done | bytes 544 | tf_op jit(solution)/shard_map/ppermute | solution.py:31
  20.2 0.0 collective-permute-done.2.refs_1_
  20.2 0.3 shard_map.120
  20.6 2.5 %collective-permute-start.5 = (bf16[16,2048]{1,0:T(8,128)(2,1)S(1)}, bf16[16,2048]{1,0:T(8,128)(2,1)S(1)}, u32[]{:S(2)}, u32[]{:S(2)}) collective-permute-start(bf16[16,2048]{1,0:T(8,128)(2,1)S(1)} %get-tuple-element.38), channel_id=1, source_target_pairs={{0,4},{4,0},{8,12},{12,8},{16,20},{20,16},{24,28},{28,24},{1,5},{5... | collective-permute-start | bytes 196616 | tf_op jit(solution)/shard_map/ppermute | solution.py:31
  23.1 2.6 %collective-permute-done.5.refs_0_ = bf16[16,2048]{1,0:T(8,128)(2,1)S(1)} collective-permute-done((bf16[16,2048]{1,0:T(8,128)(2,1)S(1)}, bf16[16,2048]{1,0:T(8,128)(2,1)S(1)}, u32[]{:S(2)}, u32[]{:S(2)}) %collective-permute-start.5) | collective-permute-done | bytes 65568 | tf_op jit(solution)/shard_map/ppermute | solution.py:31
  25.8 2.8 %collective-permute-start.6 = (bf16[16,2048]{1,0:T(8,128)(2,1)S(1)}, bf16[16,2048]{1,0:T(8,128)(2,1)S(1)}, u32[]{:S(2)}, u32[]{:S(2)}) collective-permute-start(bf16[16,2048]{1,0:T(8,128)(2,1)S(1)} %get-tuple-element.46), channel_id=1, source_target_pairs={{0,8},{4,12},{8,0},{12,4},{16,24},{20,28},{24,16},{28,20},{1,9},{5... | collective-permute-start | bytes 196616 | tf_op jit(solution)/shard_map/ppermute | solution.py:31
  28.6 2.2 %collective-permute-done.6.refs_1_ = bf16[16,2048]{1,0:T(8,128)(2,1)S(1)} collective-permute-done((bf16[16,2048]{1,0:T(8,128)(2,1)S(1)}, bf16[16,2048]{1,0:T(8,128)(2,1)S(1)}, u32[]{:S(2)}, u32[]{:S(2)}) %collective-permute-start.6) | collective-permute-done | bytes 65568 | tf_op jit(solution)/shard_map/ppermute | solution.py:31
  30.9 3.1 %collective-permute-start.7 = (bf16[16,2048]{1,0:T(8,128)(2,1)S(1)}, bf16[16,2048]{1,0:T(8,128)(2,1)S(1)}, u32[]{:S(2)}, u32[]{:S(2)}) collective-permute-start(bf16[16,2048]{1,0:T(8,128)(2,1)S(1)} %fusion.1), channel_id=1, source_target_pairs={{0,16},{4,20},{8,24},{12,28},{16,0},{20,4},{24,8},{28,12},{1,17},{... | collective-permute-start | bytes 196616 | tf_op jit(solution)/shard_map/ppermute | solution.py:31
  34.0 1.7 %shard_map.121.square_ref = bf16[64,128,256]{2,1,0:T(8,128)(2,1)S(1)} custom-call(f32[128,128]{1,0:T(8,128)S(1)} %get-tuple-element.45.impulse_ref), custom_call_target="tpu_custom_call" | custom-call | flops 134217728 | bytes 65536 | tf_op jit(solution)/shard_map/pallas_call | solution.py:337
  35.6 0.0 copy-start
  35.6 0.9 %shard_map.118 = bf16[128,2048]{1,0:T(8,128)(2,1)} custom-call(bf16[1024,128]{1,0:T(8,128)(2,1)S(1)} %get-tuple-element.31.mixed_refs_0_, bf16[1024,128]{1,0:T(8,128)(2,1)S(1)} %get-tuple-element.33.mixed_refs_1_), custom_call_target="tpu_custom_call" | custom-call | flops 33554432 | bytes 524288 | tf_op jit(solution)/shard_map/pallas_call | solution.py:337
  36.6 1.5 %shard_map.122.refs_5_ = f32[128,2048]{1,0:T(8,128)S(1)} custom-call(f32[1,128]{1,0:T(1,128)S(1)} %get-tuple-element.44.scale_ref, f32[1024,128]{1,0:T(8,128)S(1)} %get-tuple-element.36.z_refs_0_, f32[1024,128]{1,0:T(8,128)S(1)} %get-tuple-element.37.z_refs_1_, bf16[64,128,256]{2,1,0:T(8,128)(2,1)S(1)} %shard_map.121.square_ref), custom_call_target="tpu_custom_call" | custom-call | flops 134217728 | bytes 5243392 | tf_op jit(solution)/shard_map/pallas_call | solution.py:337
  38.1 0.0 collective-permute-done.7.refs_2_
  38.1 0.0 copy-done
  38.1 1.1 %shard_map.123 = bf16[128,2048]{1,0:T(8,128)(2,1)} custom-call(bf16[16,2048]{1,0:T(8,128)(2,1)S(1)} %collective-permute-done.5.refs_0_, bf16[16,2048]{1,0:T(8,128)(2,1)S(1)} %collective-permute-done.6.refs_1_, bf16[16,2048]{1,0:T(8,128)(2,1)S(1)} %collective-permute-done.7.refs_2_, f32[3,16,2048]{2,1,0:T(8,128)S(1)} %get-tuple-element.42.refs_3_, ...), custom_call_target="tpu_custom_call" | custom-call | flops 16777216 | bytes 2686976 | tf_op jit(solution)/shard_map/pallas_call | solution.py:337
  (2 shorter events, 0.1 us)
Async XLA Ops:
  1.9 12.5 %collective-permute-start = (bf16[1024,128]{1,0:T(8,128)(2,1)S(1)}, bf16[1024,128]{1,0:T(8,128)(2,1)S(1)}, u32[]{:S(2)}, u32[]{:S(2)}) collective-permute-start(bf16[1024,128]{1,0:T(8,128)(2,1)S(1)} %get-tuple-element.24.u_refs_0_), channel_id=1, source_target_pairs={{0,4},{4,8},{8,12},{12,16},{16,20},{20,24},{24,28},{28,0},{1,5},{5... | collective-permute-start | bytes 786440 | tf_op jit(solution)/shard_map/ppermute | solution.py:26
  5.0 11.1 %collective-permute-start.1 = (bf16[1024,128]{1,0:T(8,128)(2,1)S(1)}, bf16[1024,128]{1,0:T(8,128)(2,1)S(1)}, u32[]{:S(2)}, u32[]{:S(2)}) collective-permute-start(bf16[1024,128]{1,0:T(8,128)(2,1)S(1)} %shard_map.114.u_refs_1_), channel_id=1, source_target_pairs={{0,4},{4,8},{8,12},{12,16},{16,20},{20,24},{24,28},{1,5},{5,9},{9,... | collective-permute-start | bytes 786440 | tf_op jit(solution)/shard_map/ppermute | solution.py:26
  16.5 3.1 %collective-permute-start.4 = (f32[1,128]{1,0:T(1,128)S(1)}, f32[1,128]{1,0:T(1,128)S(1)}, u32[]{:S(2)}, u32[]{:S(2)}) collective-permute-start(f32[1,128]{1,0:T(1,128)S(1)} %get-tuple-element.34.refs_0_), channel_id=1, source_target_pairs={{0,3},{1,2},{2,1},{3,0},{4,7},{5,6},{6,5},{7,4},{8,11},{9,10},{10,... | collective-permute-start | bytes 1544 | tf_op jit(solution)/shard_map/ppermute | solution.py:31
  16.7 3.6 %collective-permute-start.3 = (f32[1,128]{1,0:T(1,128)S(1)}, f32[1,128]{1,0:T(1,128)S(1)}, u32[]{:S(2)}, u32[]{:S(2)}) collective-permute-start(f32[1,128]{1,0:T(1,128)S(1)} %get-tuple-element.34.refs_0_), channel_id=1, source_target_pairs={{0,2},{1,3},{2,0},{3,1},{4,6},{5,7},{6,4},{7,5},{8,10},{9,11},{10,... | collective-permute-start | bytes 1544 | tf_op jit(solution)/shard_map/ppermute | solution.py:31
  18.2 2.1 %collective-permute-start.2 = (f32[1,128]{1,0:T(1,128)S(1)}, f32[1,128]{1,0:T(1,128)S(1)}, u32[]{:S(2)}, u32[]{:S(2)}) collective-permute-start(f32[1,128]{1,0:T(1,128)S(1)} %get-tuple-element.34.refs_0_), channel_id=1, source_target_pairs={{0,1},{1,0},{2,3},{3,2},{4,5},{5,4},{6,7},{7,6},{8,9},{9,8},{10,11... | collective-permute-start | bytes 1544 | tf_op jit(solution)/shard_map/ppermute | solution.py:31
  20.6 5.2 %collective-permute-start.5 = (bf16[16,2048]{1,0:T(8,128)(2,1)S(1)}, bf16[16,2048]{1,0:T(8,128)(2,1)S(1)}, u32[]{:S(2)}, u32[]{:S(2)}) collective-permute-start(bf16[16,2048]{1,0:T(8,128)(2,1)S(1)} %get-tuple-element.38), channel_id=1, source_target_pairs={{0,4},{4,0},{8,12},{12,8},{16,20},{20,16},{24,28},{28,24},{1,5},{5... | collective-permute-start | bytes 196616 | tf_op jit(solution)/shard_map/ppermute | solution.py:31
  25.8 5.0 %collective-permute-start.6 = (bf16[16,2048]{1,0:T(8,128)(2,1)S(1)}, bf16[16,2048]{1,0:T(8,128)(2,1)S(1)}, u32[]{:S(2)}, u32[]{:S(2)}) collective-permute-start(bf16[16,2048]{1,0:T(8,128)(2,1)S(1)} %get-tuple-element.46), channel_id=1, source_target_pairs={{0,8},{4,12},{8,0},{12,4},{16,24},{20,28},{24,16},{28,20},{1,9},{5... | collective-permute-start | bytes 196616 | tf_op jit(solution)/shard_map/ppermute | solution.py:31
  30.9 7.2 %collective-permute-start.7 = (bf16[16,2048]{1,0:T(8,128)(2,1)S(1)}, bf16[16,2048]{1,0:T(8,128)(2,1)S(1)}, u32[]{:S(2)}, u32[]{:S(2)}) collective-permute-start(bf16[16,2048]{1,0:T(8,128)(2,1)S(1)} %fusion.1), channel_id=1, source_target_pairs={{0,16},{4,20},{8,24},{12,28},{16,0},{20,4},{24,8},{28,12},{1,17},{... | collective-permute-start | bytes 196616 | tf_op jit(solution)/shard_map/ppermute | solution.py:31
  35.6 2.4 %copy-start = (bf16[128,2048]{1,0:T(8,128)(2,1)S(1)}, bf16[128,2048]{1,0:T(8,128)(2,1)}, u32[]{:S(2)}) copy-start(bf16[128,2048]{1,0:T(8,128)(2,1)} %refs_6_.1) | copy-start | bytes 1572868

commit v6 on v5

--- a/solution.py
+++ b/solution.py
@@ -15,7 +15,7 @@
 SMEM = pl.BlockSpec(memory_space=pltpu.SMEM)
 HBM = pl.BlockSpec(memory_space=pltpu.HBM)
 PARTS = 4
-FIRST = 8
+FIRST = 10
 SMALL, TERMS = 0.5, 10
 SPAN = 16
 
@@ -307,13 +307,15 @@
     per = LANES // group_size
     group_of = lane_group((poles, LANES), group_size)
     empty = jnp.zeros((per * poles, LANES), BF16)
+    masks = [jnp.where(group_of == g, 1.0, 0.0).astype(BF16) for g in range(per)]
 
     def spread(i):
         at = pl.ds(i * LANES, LANES)
         carried = factor_ref[0, :, at] * got[0][:, at].astype(F32)
         for step in range(1, rounds):
             carried = carried + factor_ref[step, :, at] * got[step][:, at].astype(F32)
-        return jnp.concatenate([jnp.where(group_of == g, carried, 0.0) for g in range(per)], axis=0).astype(BF16)
+        carried = carried.astype(BF16)
+        return jnp.concatenate([carried * mask for mask in masks], axis=0)
 
     def tile(i):
         at = pl.ds(2 * i * LANES, 2 * LANES)

time: 39.3 us -> 39.9 us (1.015)
  Pallas kernels: 13.7 us -> 14.3 us
    pallas_call x11, Pallas kernels: 13.7 us -> 14.3 us  [call(): pl.pallas_call(kernel, in_specs=specs, out_specs=more.get('out_specs', ja...]
  transfers between devices with their start and end apart: 8 -> 8, of which waited for: 5 -> 5; matrix products, arithmetic and copies ran while one was open for 0% -> 0% of each run, Pallas kernels for 27% -> 29%
where the time goes in v6:
time: 39.9 us; the launch traced here: 39.7 us
  starting transfers between devices  16.7 us (42%)
  Pallas kernels  14.3 us (36%)
  waiting for transfers between devices  7.86 us (20%)
  between operations  0.75 us (2%)
    pallas_call x11, Pallas kernels, call(): pl.pallas_call(kernel, in_specs=specs, out_specs=more.get('out_specs', ja...  14.3 us
    ppermute x6, starting transfers between devices, swapped(): lax.ppermute(x, axis, [(i, i ^ bit) for i in range(peers) if i ^ bit < pe...  10.2 us
    ppermute x6, waiting for transfers between devices, swapped(): lax.ppermute(x, axis, [(i, i ^ bit) for i in range(peers) if i ^ bit < pe...  6.58 us
    ppermute x2, starting transfers between devices, passed_on(): return lax.ppermute(x, 'ctx', pairs)  6.48 us
    ppermute x2, waiting for transfers between devices, passed_on(): return lax.ppermute(x, 'ctx', pairs)  1.28 us
  transfers between devices with their start and end apart: 8, of which 5 were waited for; matrix products, arithmetic and copies ran while one was open for 0% of the time, Pallas kernels for 29%

profile of v6, /device:TPU:0, one launch (start us, length us, event | category | flops | bytes accessed | tf_op | source)
XLA Modules:
  0.0 39.7 jit_solution(2430946289312693724)
XLA Ops:
  0.6 1.3 %shard_map.113 = (bf16[1280,128]{1,0:T(8,128)(2,1)S(1)}, bf16[128,768]{1,0:T(8,128)(2,1)S(1)}, bf16[128,768]{1,0:T(8,128)(2,1)S(1)}) custom-call(bf16[128,2048]{1,0:T(8,128)(2,1)} %k_hbm.2, bf16[128,2048]{1,0:T(8,128)(2,1)} %v_hbm.1), custom_call_target="tpu_custom_call" | custom-call | flops 16777216 | bytes 1048576 | tf_op jit(solution)/shard_map/pallas_call | solution.py:339
  1.9 3.0 %collective-permute-start = (bf16[1280,128]{1,0:T(8,128)(2,1)S(1)}, bf16[1280,128]{1,0:T(8,128)(2,1)S(1)}, u32[]{:S(2)}, u32[]{:S(2)}) collective-permute-start(bf16[1280,128]{1,0:T(8,128)(2,1)S(1)} %get-tuple-element.24.u_refs_0_), channel_id=1, source_target_pairs={{0,4},{4,8},{8,12},{12,16},{16,20},{20,24},{24,28},{28,0},{1,5},{5... | collective-permute-start | bytes 983048 | tf_op jit(solution)/shard_map/ppermute | solution.py:26
  4.9 0.1 shard_map.114.u_refs_1_
  5.0 3.5 %collective-permute-start.1 = (bf16[768,128]{1,0:T(8,128)(2,1)S(1)}, bf16[768,128]{1,0:T(8,128)(2,1)S(1)}, u32[]{:S(2)}, u32[]{:S(2)}) collective-permute-start(bf16[768,128]{1,0:T(8,128)(2,1)S(1)} %shard_map.114.u_refs_1_), channel_id=1, source_target_pairs={{0,4},{4,8},{8,12},{12,16},{16,20},{20,24},{24,28},{1,5},{5,9},{9,... | collective-permute-start | bytes 589832 | tf_op jit(solution)/shard_map/ppermute | solution.py:26
  8.5 5.9 %shard_map.115 = (f32[2048,128]{1,0:T(8,128)S(1)}, f32[2048,128]{1,0:T(8,128)S(1)}, f32[2048,128]{1,0:T(8,128)S(1)}, bf16[64,128,256]{2,1,0:T(8,128)(2,1)S(1)}, ...) custom-call(s32[1]{0:T(128)} %bitcast.place_ref, ...), custom_call_target="tpu_custom_call" | custom-call | flops 1073741824 | bytes 2150404 | tf_op jit(solution)/shard_map/pallas_call | solution.py:339
  14.4 1.3 %collective-permute-done.halo_ref = bf16[1280,128]{1,0:T(8,128)(2,1)S(1)} collective-permute-done((bf16[1280,128]{1,0:T(8,128)(2,1)S(1)}, bf16[1280,128]{1,0:T(8,128)(2,1)S(1)}, u32[]{:S(2)}, u32[]{:S(2)}) %collective-permute-start) | collective-permute-done | bytes 327712 | tf_op jit(solution)/shard_map/ppermute | solution.py:26
  15.7 0.5 %shard_map.116 = (bf16[1280,128]{1,0:T(8,128)(2,1)S(1)}, f32[1280,128]{1,0:T(8,128)S(1)}, f32[1,128]{1,0:T(1,128)S(1)}) custom-call(bf16[1280,128]{1,0:T(8,128)(2,1)S(1)} %collective-permute-done.halo_ref, bf16[64,128,256]{2,1,0:T(8,128)(2,1)S(1)} %get-tuple-element.27.upper_ref, f32[2048,128]{1,0:T(8,128)S(1)} %get-tuple-element.28.base_ref, ...), custom_call_target="tpu_custom_call" | custom-call | flops 67108864 | bytes 7667712 | tf_op jit(solution)/shard_map/pallas_call | solution.py:339
  16.2 0.0 collective-permute-done.1.halo_ref
  16.2 0.4 shard_map.117
  16.5 0.3 collective-permute-start.4
  16.8 1.4 %collective-permute-start.3 = (f32[1,128]{1,0:T(1,128)S(1)}, f32[1,128]{1,0:T(1,128)S(1)}, u32[]{:S(2)}, u32[]{:S(2)}) collective-permute-start(f32[1,128]{1,0:T(1,128)S(1)} %get-tuple-element.34.refs_0_), channel_id=1, source_target_pairs={{0,2},{1,3},{2,0},{3,1},{4,6},{5,7},{6,4},{7,5},{8,10},{9,11},{10,... | collective-permute-start | bytes 1544 | tf_op jit(solution)/shard_map/ppermute | solution.py:31
  18.2 0.3 collective-permute-start.2
  18.5 0.2 shard_map.119.refs_5_
  18.7 0.9 %collective-permute-done.4.refs_3_ = f32[1,128]{1,0:T(1,128)S(1)} collective-permute-done((f32[1,128]{1,0:T(1,128)S(1)}, f32[1,128]{1,0:T(1,128)S(1)}, u32[]{:S(2)}, u32[]{:S(2)}) %collective-permute-start.4) | collective-permute-done | bytes 544 | tf_op jit(solution)/shard_map/ppermute | solution.py:31
  19.6 0.8 %collective-permute-done.3.refs_2_ = f32[1,128]{1,0:T(1,128)S(1)} collective-permute-done((f32[1,128]{1,0:T(1,128)S(1)}, f32[1,128]{1,0:T(1,128)S(1)}, u32[]{:S(2)}, u32[]{:S(2)}) %collective-permute-start.3) | collective-permute-done | bytes 544 | tf_op jit(solution)/shard_map/ppermute | solution.py:31
  20.4 0.0 collective-permute-done.2.refs_1_
  20.4 0.3 shard_map.120
  20.7 2.4 %collective-permute-start.5 = (bf16[16,2048]{1,0:T(8,128)(2,1)S(1)}, bf16[16,2048]{1,0:T(8,128)(2,1)S(1)}, u32[]{:S(2)}, u32[]{:S(2)}) collective-permute-start(bf16[16,2048]{1,0:T(8,128)(2,1)S(1)} %get-tuple-element.38), channel_id=1, source_target_pairs={{0,4},{4,0},{8,12},{12,8},{16,20},{20,16},{24,28},{28,24},{1,5},{5... | collective-permute-start | bytes 196616 | tf_op jit(solution)/shard_map/ppermute | solution.py:31
  23.1 2.6 %collective-permute-done.5.refs_0_ = bf16[16,2048]{1,0:T(8,128)(2,1)S(1)} collective-permute-done((bf16[16,2048]{1,0:T(8,128)(2,1)S(1)}, bf16[16,2048]{1,0:T(8,128)(2,1)S(1)}, u32[]{:S(2)}, u32[]{:S(2)}) %collective-permute-start.5) | collective-permute-done | bytes 65568 | tf_op jit(solution)/shard_map/ppermute | solution.py:31
  25.8 2.8 %collective-permute-start.6 = (bf16[16,2048]{1,0:T(8,128)(2,1)S(1)}, bf16[16,2048]{1,0:T(8,128)(2,1)S(1)}, u32[]{:S(2)}, u32[]{:S(2)}) collective-permute-start(bf16[16,2048]{1,0:T(8,128)(2,1)S(1)} %get-tuple-element.46), channel_id=1, source_target_pairs={{0,8},{4,12},{8,0},{12,4},{16,24},{20,28},{24,16},{28,20},{1,9},{5... | collective-permute-start | bytes 196616 | tf_op jit(solution)/shard_map/ppermute | solution.py:31
  28.5 2.2 %collective-permute-done.6.refs_1_ = bf16[16,2048]{1,0:T(8,128)(2,1)S(1)} collective-permute-done((bf16[16,2048]{1,0:T(8,128)(2,1)S(1)}, bf16[16,2048]{1,0:T(8,128)(2,1)S(1)}, u32[]{:S(2)}, u32[]{:S(2)}) %collective-permute-start.6) | collective-permute-done | bytes 65568 | tf_op jit(solution)/shard_map/ppermute | solution.py:31
  30.8 3.1 %collective-permute-start.7 = (bf16[16,2048]{1,0:T(8,128)(2,1)S(1)}, bf16[16,2048]{1,0:T(8,128)(2,1)S(1)}, u32[]{:S(2)}, u32[]{:S(2)}) collective-permute-start(bf16[16,2048]{1,0:T(8,128)(2,1)S(1)} %fusion.1), channel_id=1, source_target_pairs={{0,16},{4,20},{8,24},{12,28},{16,0},{20,4},{24,8},{28,12},{1,17},{... | collective-permute-start | bytes 196616 | tf_op jit(solution)/shard_map/ppermute | solution.py:31
  33.9 1.7 %shard_map.121.square_ref = bf16[64,128,256]{2,1,0:T(8,128)(2,1)S(1)} custom-call(f32[128,128]{1,0:T(8,128)S(1)} %get-tuple-element.45.impulse_ref), custom_call_target="tpu_custom_call" | custom-call | flops 134217728 | bytes 65536 | tf_op jit(solution)/shard_map/pallas_call | solution.py:339
  35.6 0.0 copy-start
  35.6 0.9 %shard_map.118 = bf16[128,2048]{1,0:T(8,128)(2,1)} custom-call(bf16[1280,128]{1,0:T(8,128)(2,1)S(1)} %get-tuple-element.31.mixed_refs_0_, bf16[768,128]{1,0:T(8,128)(2,1)S(1)} %get-tuple-element.33.mixed_refs_1_), custom_call_target="tpu_custom_call" | custom-call | flops 33554432 | bytes 524288 | tf_op jit(solution)/shard_map/pallas_call | solution.py:339
  36.5 2.1 %shard_map.122.refs_5_ = f32[128,2048]{1,0:T(8,128)S(1)} custom-call(f32[1,128]{1,0:T(1,128)S(1)} %get-tuple-element.44.scale_ref, f32[1280,128]{1,0:T(8,128)S(1)} %get-tuple-element.36.z_refs_0_, f32[768,128]{1,0:T(8,128)S(1)} %get-tuple-element.37.z_refs_1_, bf16[64,128,256]{2,1,0:T(8,128)(2,1)S(1)} %shard_map.121.square_ref), custom_call_target="tpu_custom_call" | custom-call | flops 134217728 | bytes 5243392 | tf_op jit(solution)/shard_map/pallas_call | solution.py:339
  38.6 0.0 collective-permute-done.7.refs_2_
  38.6 0.0 copy-done
  38.6 1.0 %shard_map.123 = bf16[128,2048]{1,0:T(8,128)(2,1)} custom-call(bf16[16,2048]{1,0:T(8,128)(2,1)S(1)} %collective-permute-done.5.refs_0_, bf16[16,2048]{1,0:T(8,128)(2,1)S(1)} %collective-permute-done.6.refs_1_, bf16[16,2048]{1,0:T(8,128)(2,1)S(1)} %collective-permute-done.7.refs_2_, f32[3,16,2048]{2,1,0:T(8,128)S(1)} %get-tuple-element.42.refs_3_, ...), custom_call_target="tpu_custom_call" | custom-call | flops 16777216 | bytes 2686976 | tf_op jit(solution)/shard_map/pallas_call | solution.py:339
  (2 shorter events, 0.1 us)
Async XLA Ops:
  1.9 13.8 %collective-permute-start = (bf16[1280,128]{1,0:T(8,128)(2,1)S(1)}, bf16[1280,128]{1,0:T(8,128)(2,1)S(1)}, u32[]{:S(2)}, u32[]{:S(2)}) collective-permute-start(bf16[1280,128]{1,0:T(8,128)(2,1)S(1)} %get-tuple-element.24.u_refs_0_), channel_id=1, source_target_pairs={{0,4},{4,8},{8,12},{12,16},{16,20},{20,24},{24,28},{28,0},{1,5},{5... | collective-permute-start | bytes 983048 | tf_op jit(solution)/shard_map/ppermute | solution.py:26
  5.0 11.1 %collective-permute-start.1 = (bf16[768,128]{1,0:T(8,128)(2,1)S(1)}, bf16[768,128]{1,0:T(8,128)(2,1)S(1)}, u32[]{:S(2)}, u32[]{:S(2)}) collective-permute-start(bf16[768,128]{1,0:T(8,128)(2,1)S(1)} %shard_map.114.u_refs_1_), channel_id=1, source_target_pairs={{0,4},{4,8},{8,12},{12,16},{16,20},{20,24},{24,28},{1,5},{5,9},{9,... | collective-permute-start | bytes 589832 | tf_op jit(solution)/shard_map/ppermute | solution.py:26
  16.5 3.1 %collective-permute-start.4 = (f32[1,128]{1,0:T(1,128)S(1)}, f32[1,128]{1,0:T(1,128)S(1)}, u32[]{:S(2)}, u32[]{:S(2)}) collective-permute-start(f32[1,128]{1,0:T(1,128)S(1)} %get-tuple-element.34.refs_0_), channel_id=1, source_target_pairs={{0,3},{1,2},{2,1},{3,0},{4,7},{5,6},{6,5},{7,4},{8,11},{9,10},{10,... | collective-permute-start | bytes 1544 | tf_op jit(solution)/shard_map/ppermute | solution.py:31
  16.8 3.6 %collective-permute-start.3 = (f32[1,128]{1,0:T(1,128)S(1)}, f32[1,128]{1,0:T(1,128)S(1)}, u32[]{:S(2)}, u32[]{:S(2)}) collective-permute-start(f32[1,128]{1,0:T(1,128)S(1)} %get-tuple-element.34.refs_0_), channel_id=1, source_target_pairs={{0,2},{1,3},{2,0},{3,1},{4,6},{5,7},{6,4},{7,5},{8,10},{9,11},{10,... | collective-permute-start | bytes 1544 | tf_op jit(solution)/shard_map/ppermute | solution.py:31
  18.2 2.2 %collective-permute-start.2 = (f32[1,128]{1,0:T(1,128)S(1)}, f32[1,128]{1,0:T(1,128)S(1)}, u32[]{:S(2)}, u32[]{:S(2)}) collective-permute-start(f32[1,128]{1,0:T(1,128)S(1)} %get-tuple-element.34.refs_0_), channel_id=1, source_target_pairs={{0,1},{1,0},{2,3},{3,2},{4,5},{5,4},{6,7},{7,6},{8,9},{9,8},{10,11... | collective-permute-start | bytes 1544 | tf_op jit(solution)/shard_map/ppermute | solution.py:31
  20.7 5.0 %collective-permute-start.5 = (bf16[16,2048]{1,0:T(8,128)(2,1)S(1)}, bf16[16,2048]{1,0:T(8,128)(2,1)S(1)}, u32[]{:S(2)}, u32[]{:S(2)}) collective-permute-start(bf16[16,2048]{1,0:T(8,128)(2,1)S(1)} %get-tuple-element.38), channel_id=1, source_target_pairs={{0,4},{4,0},{8,12},{12,8},{16,20},{20,16},{24,28},{28,24},{1,5},{5... | collective-permute-start | bytes 196616 | tf_op jit(solution)/shard_map/ppermute | solution.py:31
  25.8 5.0 %collective-permute-start.6 = (bf16[16,2048]{1,0:T(8,128)(2,1)S(1)}, bf16[16,2048]{1,0:T(8,128)(2,1)S(1)}, u32[]{:S(2)}, u32[]{:S(2)}) collective-permute-start(bf16[16,2048]{1,0:T(8,128)(2,1)S(1)} %get-tuple-element.46), channel_id=1, source_target_pairs={{0,8},{4,12},{8,0},{12,4},{16,24},{20,28},{24,16},{28,20},{1,9},{5... | collective-permute-start | bytes 196616 | tf_op jit(solution)/shard_map/ppermute | solution.py:31
  30.8 7.8 %collective-permute-start.7 = (bf16[16,2048]{1,0:T(8,128)(2,1)S(1)}, bf16[16,2048]{1,0:T(8,128)(2,1)S(1)}, u32[]{:S(2)}, u32[]{:S(2)}) collective-permute-start(bf16[16,2048]{1,0:T(8,128)(2,1)S(1)} %fusion.1), channel_id=1, source_target_pairs={{0,16},{4,20},{8,24},{12,28},{16,0},{20,4},{24,8},{28,12},{1,17},{... | collective-permute-start | bytes 196616 | tf_op jit(solution)/shard_map/ppermute | solution.py:31
  35.6 3.0 %copy-start = (bf16[128,2048]{1,0:T(8,128)(2,1)S(1)}, bf16[128,2048]{1,0:T(8,128)(2,1)}, u32[]{:S(2)}) copy-start(bf16[128,2048]{1,0:T(8,128)(2,1)} %refs_6_.1) | copy-start | bytes 1572868
